TPU v7x, 512 devices: a whole 4x8x8 slice. The times are simulated.
512 devices in a mesh: lat: 32 (over x, y), lon: 16 (over z, core).
Axes of the slice: x: 4, y: 8, z: 8, core: 2. Of those that a mesh axis runs over, the one named last changes fastest.
Arguments:
- tracer: float32 [8, 1024, 4096], P(None, 'lat', 'lon'), may hold values from -6 to 6
- thickness: float32 [8, 1024, 4096], P(None, 'lat', 'lon'), may hold values from 0.5 to 2
- land_mask: int32 [8, 1024, 4096], P(None, 'lat', 'lon'), may hold values 0 or 1
- zonal_vel: float32 [8, 1024, 4096], P(None, 'lat', 'lon'), may hold values from -2 to 2
- meridional_vel: float32 [8, 1024, 4096], P(None, 'lat', 'lon'), may hold values from -2 to 2
- surface: float32 [1024, 4096], P('lat', 'lon'), may hold values from -3 to 3
- zonal_baro: float32 [1024, 4096], P('lat', 'lon'), may hold values from -2 to 2
- merid_baro: float32 [1024, 4096], P('lat', 'lon'), may hold values from -2 to 2
Outputs:
- tracer_next: float32 [8, 1024, 4096], P(None, 'lat', 'lon')
- surface_next: float32 [1024, 4096], P('lat', 'lon')
- zonal_next: float32 [1024, 4096], P('lat', 'lon')
- merid_next: float32 [1024, 4096], P('lat', 'lon')
All inputs are finite; a program needn't handle non-finite values. No bound on the sum of `land_mask` on one device may be relied on, other than what follows from the above.
Results may differ from a plain program's by a relative error of at most 0.00002.
Values sent between devices are 32-bit elements; how exact they have to be, the bound alone decides.
A program may use at most 64 MiB of HBM per device.

v0:
```python
import jax
import jax.numpy as jnp
from jax import lax
from jax.sharding import PartitionSpec as P

SUB = 8


def swapped(value, axis, bit):
    mask = 2**bit
    pairs = [(source, source ^ mask) for source in range(lax.axis_size(axis))]
    return lax.ppermute(value, axis, pairs)


def extended_2(block, sides, width):
    for axis, dim in sides:
        count = lax.axis_size(axis)
        forward = [(i, i + 1) for i in range(count - 1)]
        forward.append((count - 1, 0))
        backward = [(target, source) for source, target in forward]
        low = lax.ppermute(
            lax.slice_in_dim(block, block.shape[dim] - width, None, axis=dim), axis, forward
        )
        high = lax.ppermute(lax.slice_in_dim(block, 0, width, axis=dim), axis, backward)
        block = jnp.concatenate([low, block, high], axis=dim)
    return block


def tracer_update(padded_t, padded_h, padded_u, padded_v, wet_cells, thickness):
    center_t = padded_t[:, 1:-1, 1:-1]
    center_h = padded_h[:, 1:-1, 1:-1]
    east_depth = jnp.minimum(padded_h[:, 1:-1, :-1], padded_h[:, 1:-1, 1:])
    east_flux = east_depth * (
        0.25
        * (padded_u[:, 1:-1, :-1] + padded_u[:, 1:-1, 1:])
        * (padded_t[:, 1:-1, :-1] + padded_t[:, 1:-1, 1:])
        - 0.1 * (padded_t[:, 1:-1, 1:] - padded_t[:, 1:-1, :-1])
    )
    north_depth = jnp.minimum(padded_h[:, :-1, 1:-1], padded_h[:, 1:, 1:-1])
    north_flux = north_depth * (
        0.25
        * (padded_v[:, :-1, 1:-1] + padded_v[:, 1:, 1:-1])
        * (padded_t[:, :-1, 1:-1] + padded_t[:, 1:, 1:-1])
        - 0.1 * (padded_t[:, 1:, 1:-1] - padded_t[:, :-1, 1:-1])
    )
    vertical = 0.2 * jnp.minimum(center_h[:-1], center_h[1:]) * (center_t[1:] - center_t[:-1])
    zero_level = jnp.zeros_like(center_t[:1])
    vertical_div = jnp.concatenate([vertical, zero_level], axis=0) - jnp.concatenate(
        [zero_level, vertical], axis=0
    )
    tendency = (
        vertical_div
        - (east_flux[:, :, 1:] - east_flux[:, :, :-1])
        - (north_flux[:, 1:, :] - north_flux[:, :-1, :])
    )
    return center_t + 0.2 * wet_cells / thickness * tendency


def subcycle(height, zonal, merid, depth, force_u, force_v):
    wet = jnp.minimum(2.0 * depth, 1.0)
    east_flux = jnp.minimum(depth[:, :-1], depth[:, 1:]) * 0.5 * (zonal[:, :-1] + zonal[:, 1:])
    north_flux = jnp.minimum(depth[:-1], depth[1:]) * 0.5 * (merid[:-1] + merid[1:])
    divergence = (
        east_flux[1:-1, 1:] - east_flux[1:-1, :-1] + north_flux[1:, 1:-1] - north_flux[:-1, 1:-1]
    )
    height_new = height[1:-1, 1:-1] - 0.2 * wet[1:-1, 1:-1] * divergence
    slope_x = 0.5 * (height_new[1:-1, 2:] - height_new[1:-1, :-2])
    slope_y = 0.5 * (height_new[2:, 1:-1] - height_new[:-2, 1:-1])
    inner = wet[2:-2, 2:-2]
    zonal_new = inner * (zonal[2:-2, 2:-2] - 0.2 * 0.5 * slope_x + 0.2 * force_u[2:-2, 2:-2])
    merid_new = inner * (merid[2:-2, 2:-2] - 0.2 * 0.5 * slope_y + 0.2 * force_v[2:-2, 2:-2])
    return (height_new[1:-1, 1:-1], zonal_new, merid_new)


def mirror(piece):
    bit_count = lax.axis_size("lon").bit_length() - 1
    bit_order = list(range(bit_count))
    result = piece
    for bit_index in bit_order:
        result = swapped(result, "lon", bit_index)
    return result


def extend(extended, rows, width, signs):
    band = lax.axis_index("lat")
    last_band = lax.axis_size("lat") - 1
    piece = signs[:, None, None] * jnp.flip(extended[:, rows : rows + width, :], (1, 2))
    folded = mirror(piece)
    upper = jnp.where(band == last_band, folded, extended[:, rows + width :, :])
    lower = jnp.where(band == 0, jnp.zeros_like(extended[:, :width, :]), extended[:, :width, :])
    return jnp.concatenate([lower, extended[:, width : rows + width, :], upper], axis=1)


def on_device(
    tracer, thickness, land_mask, zonal_vel, meridional_vel, surface, zonal_baro, merid_baro
):
    levels, rows, columns = tracer.shape
    wet_cells = land_mask.astype(jnp.float32)
    wet_thick = wet_cells * thickness
    depth = jnp.sum(wet_thick, axis=0)
    force_u = 0.05 * jnp.sum(wet_thick * zonal_vel, axis=0)
    force_v = 0.05 * jnp.sum(wet_thick * meridional_vel, axis=0)
    stacked = jnp.concatenate([tracer, wet_thick, zonal_vel, meridional_vel], axis=0)
    tracer_signs = jnp.concatenate(
        [jnp.ones((2 * levels,), jnp.float32), -jnp.ones((2 * levels,), jnp.float32)]
    )
    padded = extended_2(stacked, (("lat", 1), ("lon", 2)), 1)
    padded = extend(padded, rows, 1, tracer_signs)
    padded = padded.reshape(4, levels, rows + 2, columns + 2)
    tracer_next = tracer_update(padded[0], padded[1], padded[2], padded[3], wet_cells, thickness)
    per_exchange = 1
    width = 2 * per_exchange
    state_signs = jnp.array([1.0, -1.0, -1.0], jnp.float32)
    column_fields = jnp.stack([depth, force_u, force_v])
    column_pad = extended_2(column_fields, (("lat", 1), ("lon", 2)), width)
    column_pad = extend(column_pad, rows, width, state_signs)
    state = jnp.stack([surface, zonal_baro, merid_baro])
    for number in range(SUB // per_exchange):
        state_pad = extended_2(state, (("lat", 1), ("lon", 2)), width)
        state_pad = extend(state_pad, rows, width, state_signs)
        height, zonal, merid = (state_pad[0], state_pad[1], state_pad[2])
        depth_win, force_u_win, force_v_win = (column_pad[0], column_pad[1], column_pad[2])
        height, zonal, merid = subcycle(height, zonal, merid, depth_win, force_u_win, force_v_win)
        depth_win = depth_win[2:-2, 2:-2]
        force_u_win = force_u_win[2:-2, 2:-2]
        force_v_win = force_v_win[2:-2, 2:-2]
        state = jnp.stack([height, zonal, merid])
    return (tracer_next, state[0], state[1], state[2])


def solution(mesh):
    return jax.shard_map(
        on_device,
        mesh=mesh,
        in_specs=(
            P(None, "lat", "lon"),
            P(None, "lat", "lon"),
            P(None, "lat", "lon"),
            P(None, "lat", "lon"),
            P(None, "lat", "lon"),
            P("lat", "lon"),
            P("lat", "lon"),
            P("lat", "lon"),
        ),
        out_specs=(P(None, "lat", "lon"), P("lat", "lon"), P("lat", "lon"), P("lat", "lon")),
        check_vma=False,
    )
```

profile of v0, /device:TPU:64, one launch (start us, length us, event | category | flops | bytes accessed | tf_op | source)
XLA Modules:
  0.0 413.4 jit_solution(6986680148471991243)
XLA Ops:
  4.9 6.1 %collective-permute-start.9 = (f32[3,2,256]{2,1,0:T(2,128)S(1)}, f32[3,2,256]{2,1,0:T(2,128)S(1)}, u32[]{:S(2)}, u32[]{:S(2)}) collective-permute-start(f32[3,2,256]{2,1,0:T(2,128)S(1)} %get-tuple-element.162), channel_id=1, source_target_pairs={{16,0},{32,16},{48,32},{64,48},{80,64},{96,80},{112,96},{128,112},... | collective-permute-start | bytes 18440 | tf_op jit(solution)/shard_map/ppermute | solution.py:24
  15.6 7.2 %collective-permute-start.17 = (f32[3,2,256]{2,1,0:T(2,128)S(1)}, f32[3,2,256]{2,1,0:T(2,128)S(1)}, u32[]{:S(2)}, u32[]{:S(2)}) collective-permute-start(f32[3,2,256]{2,1,0:T(2,128)S(1)} %get-tuple-element.160), channel_id=1, source_target_pairs={{16,0},{32,16},{48,32},{64,48},{80,64},{96,80},{112,96},{128,112},... | collective-permute-start | bytes 18440 | tf_op jit(solution)/shard_map/ppermute | solution.py:24
  35.4 7.0 %collective-permute-start.21 = (f32[3,2,260]{2,1,0:T(2,128)S(1)}, f32[3,2,260]{2,1,0:T(2,128)S(1)}, u32[]{:S(2)}, u32[]{:S(2)}) collective-permute-start(f32[3,2,260]{2,1,0:T(2,128)S(1)} %collective-permute-done.20), channel_id=1, source_target_pairs={{0,2},{1,3},{2,0},{3,1},{4,6},{5,7},{6,4},{7,5},{8,10},{9,11},{10,... | collective-permute-start | bytes 18728 | tf_op jit(solution)/shard_map/ppermute | solution.py:12
  44.4 6.6 %collective-permute-start.22 = (f32[3,2,260]{2,1,0:T(2,128)S(1)}, f32[3,2,260]{2,1,0:T(2,128)S(1)}, u32[]{:S(2)}, u32[]{:S(2)}) collective-permute-start(f32[3,2,260]{2,1,0:T(2,128)S(1)} %collective-permute-done.21), channel_id=1, source_target_pairs={{0,4},{1,5},{2,6},{3,7},{4,0},{5,1},{6,2},{7,3},{8,12},{9,13},{10,... | collective-permute-start | bytes 18728 | tf_op jit(solution)/shard_map/ppermute | solution.py:12
  57.7 5.5 %collective-permute-start.15 = (f32[3,2,260]{2,1,0:T(2,128)S(1)}, f32[3,2,260]{2,1,0:T(2,128)S(1)}, u32[]{:S(2)}, u32[]{:S(2)}) collective-permute-start(f32[3,2,260]{2,1,0:T(2,128)S(1)} %collective-permute-done.14), channel_id=1, source_target_pairs={{0,8},{1,9},{2,10},{3,11},{4,12},{5,13},{6,14},{7,15},{8,0},{9,1},... | collective-permute-start | bytes 18728 | tf_op jit(solution)/shard_map/ppermute | solution.py:12
  71.3 7.2 %collective-permute-start.25 = (f32[3,2,256]{2,1,0:T(2,128)S(1)}, f32[3,2,256]{2,1,0:T(2,128)S(1)}, u32[]{:S(2)}, u32[]{:S(2)}) collective-permute-start(f32[3,2,256]{2,1,0:T(2,128)S(1)} %get-tuple-element.158), channel_id=1, source_target_pairs={{16,0},{32,16},{48,32},{64,48},{80,64},{96,80},{112,96},{128,112},... | collective-permute-start | bytes 18440 | tf_op jit(solution)/shard_map/ppermute | solution.py:24
  93.9 5.9 %collective-permute-start.30 = (f32[3,2,260]{2,1,0:T(2,128)S(1)}, f32[3,2,260]{2,1,0:T(2,128)S(1)}, u32[]{:S(2)}, u32[]{:S(2)}) collective-permute-start(f32[3,2,260]{2,1,0:T(2,128)S(1)} %collective-permute-done.29), channel_id=1, source_target_pairs={{0,4},{1,5},{2,6},{3,7},{4,0},{5,1},{6,2},{7,3},{8,12},{9,13},{10,... | collective-permute-start | bytes 18728 | tf_op jit(solution)/shard_map/ppermute | solution.py:12
  101.4 4.6 %collective-permute-start.31 = (f32[3,2,260]{2,1,0:T(2,128)S(1)}, f32[3,2,260]{2,1,0:T(2,128)S(1)}, u32[]{:S(2)}, u32[]{:S(2)}) collective-permute-start(f32[3,2,260]{2,1,0:T(2,128)S(1)} %collective-permute-done.30), channel_id=1, source_target_pairs={{0,8},{1,9},{2,10},{3,11},{4,12},{5,13},{6,14},{7,15},{8,0},{9,1},... | collective-permute-start | bytes 18728 | tf_op jit(solution)/shard_map/ppermute | solution.py:12
  106.2 4.7 %collective-permute-done.31 = f32[3,2,260]{2,1,0:T(2,128)S(1)} collective-permute-done((f32[3,2,260]{2,1,0:T(2,128)S(1)}, f32[3,2,260]{2,1,0:T(2,128)S(1)}, u32[]{:S(2)}, u32[]{:S(2)}) %collective-permute-start.31) | collective-permute-done | bytes 6272 | tf_op jit(solution)/shard_map/ppermute | solution.py:12
  114.5 7.5 %collective-permute-start.33 = (f32[3,2,256]{2,1,0:T(2,128)S(1)}, f32[3,2,256]{2,1,0:T(2,128)S(1)}, u32[]{:S(2)}, u32[]{:S(2)}) collective-permute-start(f32[3,2,256]{2,1,0:T(2,128)S(1)} %get-tuple-element.156), channel_id=1, source_target_pairs={{16,0},{32,16},{48,32},{64,48},{80,64},{96,80},{112,96},{128,112},... | collective-permute-start | bytes 18440 | tf_op jit(solution)/shard_map/ppermute | solution.py:24
  137.4 4.8 %collective-permute-start.38 = (f32[3,2,260]{2,1,0:T(2,128)S(1)}, f32[3,2,260]{2,1,0:T(2,128)S(1)}, u32[]{:S(2)}, u32[]{:S(2)}) collective-permute-start(f32[3,2,260]{2,1,0:T(2,128)S(1)} %collective-permute-done.37), channel_id=1, source_target_pairs={{0,4},{1,5},{2,6},{3,7},{4,0},{5,1},{6,2},{7,3},{8,12},{9,13},{10,... | collective-permute-start | bytes 18728 | tf_op jit(solution)/shard_map/ppermute | solution.py:12
  143.9 5.0 %collective-permute-start.39 = (f32[3,2,260]{2,1,0:T(2,128)S(1)}, f32[3,2,260]{2,1,0:T(2,128)S(1)}, u32[]{:S(2)}, u32[]{:S(2)}) collective-permute-start(f32[3,2,260]{2,1,0:T(2,128)S(1)} %collective-permute-done.38), channel_id=1, source_target_pairs={{0,8},{1,9},{2,10},{3,11},{4,12},{5,13},{6,14},{7,15},{8,0},{9,1},... | collective-permute-start | bytes 18728 | tf_op jit(solution)/shard_map/ppermute | solution.py:12
  156.9 7.5 %collective-permute-start.41 = (f32[3,2,256]{2,1,0:T(2,128)S(1)}, f32[3,2,256]{2,1,0:T(2,128)S(1)}, u32[]{:S(2)}, u32[]{:S(2)}) collective-permute-start(f32[3,2,256]{2,1,0:T(2,128)S(1)} %get-tuple-element.154), channel_id=1, source_target_pairs={{16,0},{32,16},{48,32},{64,48},{80,64},{96,80},{112,96},{128,112},... | collective-permute-start | bytes 18440 | tf_op jit(solution)/shard_map/ppermute | solution.py:24
  191.7 4.7 %collective-permute-done.47 = f32[3,2,260]{2,1,0:T(2,128)S(1)} collective-permute-done((f32[3,2,260]{2,1,0:T(2,128)S(1)}, f32[3,2,260]{2,1,0:T(2,128)S(1)}, u32[]{:S(2)}, u32[]{:S(2)}) %collective-permute-start.47) | collective-permute-done | bytes 6272 | tf_op jit(solution)/shard_map/ppermute | solution.py:12
  199.9 7.5 %collective-permute-start.49 = (f32[3,2,256]{2,1,0:T(2,128)S(1)}, f32[3,2,256]{2,1,0:T(2,128)S(1)}, u32[]{:S(2)}, u32[]{:S(2)}) collective-permute-start(f32[3,2,256]{2,1,0:T(2,128)S(1)} %get-tuple-element.152), channel_id=1, source_target_pairs={{16,0},{32,16},{48,32},{64,48},{80,64},{96,80},{112,96},{128,112},... | collective-permute-start | bytes 18440 | tf_op jit(solution)/shard_map/ppermute | solution.py:24
  234.1 4.7 %collective-permute-done.55 = f32[3,2,260]{2,1,0:T(2,128)S(1)} collective-permute-done((f32[3,2,260]{2,1,0:T(2,128)S(1)}, f32[3,2,260]{2,1,0:T(2,128)S(1)}, u32[]{:S(2)}, u32[]{:S(2)}) %collective-permute-start.55) | collective-permute-done | bytes 6272 | tf_op jit(solution)/shard_map/ppermute | solution.py:12
  242.3 7.5 %collective-permute-start.57 = (f32[3,2,256]{2,1,0:T(2,128)S(1)}, f32[3,2,256]{2,1,0:T(2,128)S(1)}, u32[]{:S(2)}, u32[]{:S(2)}) collective-permute-start(f32[3,2,256]{2,1,0:T(2,128)S(1)} %get-tuple-element.150), channel_id=1, source_target_pairs={{16,0},{32,16},{48,32},{64,48},{80,64},{96,80},{112,96},{128,112},... | collective-permute-start | bytes 18440 | tf_op jit(solution)/shard_map/ppermute | solution.py:24
  255.0 7.5 %collective-permute-start.1 = (f32[32,1,256]{2,0,1:T(8,128)S(1)}, f32[32,1,256]{2,0,1:T(8,128)S(1)}, u32[]{:S(2)}, u32[]{:S(2)}) collective-permute-start(f32[32,1,256]{2,0,1:T(8,128)S(1)} %get-tuple-element.37), channel_id=1, source_target_pairs={{16,0},{32,16},{48,32},{64,48},{80,64},{96,80},{112,96},{128,112},... | collective-permute-start | bytes 98312 | tf_op jit(solution)/shard_map/ppermute | solution.py:24
  287.1 4.7 %collective-permute-done.63 = f32[3,2,260]{2,1,0:T(2,128)S(1)} collective-permute-done((f32[3,2,260]{2,1,0:T(2,128)S(1)}, f32[3,2,260]{2,1,0:T(2,128)S(1)}, u32[]{:S(2)}, u32[]{:S(2)}) %collective-permute-start.63) | collective-permute-done | bytes 6272 | tf_op jit(solution)/shard_map/ppermute | solution.py:12
  295.9 7.2 %collective-permute-start.65 = (f32[3,2,256]{2,1,0:T(2,128)}, f32[3,2,256]{2,1,0:T(2,128)}, u32[]{:S(2)}, u32[]{:S(2)}) collective-permute-start(f32[3,2,256]{2,1,0:T(2,128)} %get-tuple-element.148), channel_id=1, source_target_pairs={{16,0},{32,16},{48,32},{64,48},{80,64},{96,80},{112,96},{128,112},... | collective-permute-start | bytes 18440 | tf_op jit(solution)/shard_map/ppermute | solution.py:24
  320.7 5.0 %collective-permute-start.69 = (f32[3,2,260]{2,1,0:T(2,128)S(1)}, f32[3,2,260]{2,1,0:T(2,128)S(1)}, u32[]{:S(2)}, u32[]{:S(2)}) collective-permute-start(f32[3,2,260]{2,1,0:T(2,128)S(1)} %collective-permute-done.68), channel_id=1, source_target_pairs={{0,2},{1,3},{2,0},{3,1},{4,6},{5,7},{6,4},{7,5},{8,10},{9,11},{10,... | collective-permute-start | bytes 18728 | tf_op jit(solution)/shard_map/ppermute | solution.py:12
  361.0 7.2 %collective-permute-start.73 = (f32[3,2,256]{2,1,0:T(2,128)S(1)}, f32[3,2,256]{2,1,0:T(2,128)S(1)}, u32[]{:S(2)}, u32[]{:S(2)}) collective-permute-start(f32[3,2,256]{2,1,0:T(2,128)S(1)} %get-tuple-element.146), channel_id=1, source_target_pairs={{16,0},{32,16},{48,32},{64,48},{80,64},{96,80},{112,96},{128,112},... | collective-permute-start | bytes 18440 | tf_op jit(solution)/shard_map/ppermute | solution.py:24
  377.7 4.9 %collective-permute-start.7 = (f32[32,1,258]{2,0,1:T(8,128)}, f32[32,1,258]{2,0,1:T(8,128)S(1)}, u32[]{:S(2)}, u32[]{:S(2)}) collective-permute-start(f32[32,1,258]{2,0,1:T(8,128)} %collective-permute-done.6), channel_id=1, source_target_pairs={{0,8},{1,9},{2,10},{3,11},{4,12},{5,13},{6,14},{7,15},{8,0},{9,1},... | collective-permute-start | bytes 99080 | tf_op jit(solution)/shard_map/ppermute | solution.py:12
  404.9 5.0 %collective-permute-done.79 = f32[3,2,260]{2,1,0:T(2,128)S(1)} collective-permute-done((f32[3,2,260]{2,1,0:T(2,128)S(1)}, f32[3,2,260]{2,1,0:T(2,128)S(1)}, u32[]{:S(2)}, u32[]{:S(2)}) %collective-permute-start.79) | collective-permute-done | bytes 6272 | tf_op jit(solution)/shard_map/ppermute | solution.py:12
  (413 shorter events, 264.9 us)
Async XLA Ops:
  1.4 21.5 %collective-permute-start.8 = (f32[3,2,256]{2,1,0:T(2,128)S(1)}, f32[3,2,256]{2,1,0:T(2,128)S(1)}, u32[]{:S(2)}, u32[]{:S(2)}) collective-permute-start(f32[3,2,256]{2,1,0:T(2,128)S(1)} %get-tuple-element.161), channel_id=1, source_target_pairs={{0,16},{16,32},{32,48},{48,64},{64,80},{80,96},{96,112},{112,128},... | collective-permute-start | bytes 18440 | tf_op jit(solution)/shard_map/ppermute | solution.py:21
  4.9 18.0 %collective-permute-start.9 = (f32[3,2,256]{2,1,0:T(2,128)S(1)}, f32[3,2,256]{2,1,0:T(2,128)S(1)}, u32[]{:S(2)}, u32[]{:S(2)}) collective-permute-start(f32[3,2,256]{2,1,0:T(2,128)S(1)} %get-tuple-element.162), channel_id=1, source_target_pairs={{16,0},{32,16},{48,32},{64,48},{80,64},{96,80},{112,96},{128,112},... | collective-permute-start | bytes 18440 | tf_op jit(solution)/shard_map/ppermute | solution.py:24
  13.7 11.1 %collective-permute-start.16 = (f32[3,2,256]{2,1,0:T(2,128)S(1)}, f32[3,2,256]{2,1,0:T(2,128)S(1)}, u32[]{:S(2)}, u32[]{:S(2)}) collective-permute-start(f32[3,2,256]{2,1,0:T(2,128)S(1)} %get-tuple-element.159), channel_id=1, source_target_pairs={{0,16},{16,32},{32,48},{48,64},{64,80},{80,96},{96,112},{112,128},... | collective-permute-start | bytes 18440 | tf_op jit(solution)/shard_map/ppermute | solution.py:21
  53.2 10.0 %collective-permute-start.23 = (f32[3,2,260]{2,1,0:T(2,128)S(1)}, f32[3,2,260]{2,1,0:T(2,128)S(1)}, u32[]{:S(2)}, u32[]{:S(2)}) collective-permute-start(f32[3,2,260]{2,1,0:T(2,128)S(1)} %collective-permute-done.22), channel_id=1, source_target_pairs={{0,8},{1,9},{2,10},{3,11},{4,12},{5,13},{6,14},{7,15},{8,0},{9,1},... | collective-permute-start | bytes 18728 | tf_op jit(solution)/shard_map/ppermute | solution.py:12
  57.7 9.5 %collective-permute-start.15 = (f32[3,2,260]{2,1,0:T(2,128)S(1)}, f32[3,2,260]{2,1,0:T(2,128)S(1)}, u32[]{:S(2)}, u32[]{:S(2)}) collective-permute-start(f32[3,2,260]{2,1,0:T(2,128)S(1)} %collective-permute-done.14), channel_id=1, source_target_pairs={{0,8},{1,9},{2,10},{3,11},{4,12},{5,13},{6,14},{7,15},{8,0},{9,1},... | collective-permute-start | bytes 18728 | tf_op jit(solution)/shard_map/ppermute | solution.py:12
  101.4 9.5 %collective-permute-start.31 = (f32[3,2,260]{2,1,0:T(2,128)S(1)}, f32[3,2,260]{2,1,0:T(2,128)S(1)}, u32[]{:S(2)}, u32[]{:S(2)}) collective-permute-start(f32[3,2,260]{2,1,0:T(2,128)S(1)} %collective-permute-done.30), channel_id=1, source_target_pairs={{0,8},{1,9},{2,10},{3,11},{4,12},{5,13},{6,14},{7,15},{8,0},{9,1},... | collective-permute-start | bytes 18728 | tf_op jit(solution)/shard_map/ppermute | solution.py:12
  143.9 9.5 %collective-permute-start.39 = (f32[3,2,260]{2,1,0:T(2,128)S(1)}, f32[3,2,260]{2,1,0:T(2,128)S(1)}, u32[]{:S(2)}, u32[]{:S(2)}) collective-permute-start(f32[3,2,260]{2,1,0:T(2,128)S(1)} %collective-permute-done.38), channel_id=1, source_target_pairs={{0,8},{1,9},{2,10},{3,11},{4,12},{5,13},{6,14},{7,15},{8,0},{9,1},... | collective-permute-start | bytes 18728 | tf_op jit(solution)/shard_map/ppermute | solution.py:12
  186.9 9.5 %collective-permute-start.47 = (f32[3,2,260]{2,1,0:T(2,128)S(1)}, f32[3,2,260]{2,1,0:T(2,128)S(1)}, u32[]{:S(2)}, u32[]{:S(2)}) collective-permute-start(f32[3,2,260]{2,1,0:T(2,128)S(1)} %collective-permute-done.46), channel_id=1, source_target_pairs={{0,8},{1,9},{2,10},{3,11},{4,12},{5,13},{6,14},{7,15},{8,0},{9,1},... | collective-permute-start | bytes 18728 | tf_op jit(solution)/shard_map/ppermute | solution.py:12
  229.3 9.5 %collective-permute-start.55 = (f32[3,2,260]{2,1,0:T(2,128)S(1)}, f32[3,2,260]{2,1,0:T(2,128)S(1)}, u32[]{:S(2)}, u32[]{:S(2)}) collective-permute-start(f32[3,2,260]{2,1,0:T(2,128)S(1)} %collective-permute-done.54), channel_id=1, source_target_pairs={{0,8},{1,9},{2,10},{3,11},{4,12},{5,13},{6,14},{7,15},{8,0},{9,1},... | collective-permute-start | bytes 18728 | tf_op jit(solution)/shard_map/ppermute | solution.py:12
  240.4 9.6 %collective-permute-start.56 = (f32[3,2,256]{2,1,0:T(2,128)S(1)}, f32[3,2,256]{2,1,0:T(2,128)S(1)}, u32[]{:S(2)}, u32[]{:S(2)}) collective-permute-start(f32[3,2,256]{2,1,0:T(2,128)S(1)} %get-tuple-element.149), channel_id=1, source_target_pairs={{0,16},{16,32},{32,48},{48,64},{64,80},{80,96},{96,112},{112,128},... | collective-permute-start | bytes 18440 | tf_op jit(solution)/shard_map/ppermute | solution.py:21
  251.3 11.2 %collective-permute-start.58 = (f32[3,36,2]{2,1,0:T(8,128)S(1)}, f32[3,36,2]{2,1,0:T(8,128)S(1)}, u32[]{:S(2)}, u32[]{:S(2)}) collective-permute-start(f32[3,36,2]{2,1,0:T(8,128)S(1)} %get-tuple-element.131), channel_id=1, source_target_pairs={{0,1},{1,2},{2,3},{3,4},{4,5},{5,6},{6,7},{7,8},{8,9},{9,10},{10,1... | collective-permute-start | bytes 2600 | tf_op jit(solution)/shard_map/ppermute | solution.py:21
  251.3 11.2 %collective-permute-start.59 = (f32[3,36,2]{2,1,0:T(8,128)S(1)}, f32[3,36,2]{2,1,0:T(8,128)S(1)}, u32[]{:S(2)}, u32[]{:S(2)}) collective-permute-start(f32[3,36,2]{2,1,0:T(8,128)S(1)} %get-tuple-element.132), channel_id=1, source_target_pairs={{1,0},{2,1},{3,2},{4,3},{5,4},{6,5},{7,6},{8,7},{9,8},{10,9},{11,1... | collective-permute-start | bytes 2600 | tf_op jit(solution)/shard_map/ppermute | solution.py:24
  253.1 17.0 %collective-permute-start = (f32[32,1,256]{2,0,1:T(8,128)S(1)}, f32[32,1,256]{2,0,1:T(8,128)S(1)}, u32[]{:S(2)}, u32[]{:S(2)}) collective-permute-start(f32[32,1,256]{2,0,1:T(8,128)S(1)} %get-tuple-element.36), channel_id=1, source_target_pairs={{0,16},{16,32},{32,48},{48,64},{64,80},{80,96},{96,112},{112,128},... | collective-permute-start | bytes 98312 | tf_op jit(solution)/shard_map/ppermute | solution.py:21
  255.0 15.1 %collective-permute-start.1 = (f32[32,1,256]{2,0,1:T(8,128)S(1)}, f32[32,1,256]{2,0,1:T(8,128)S(1)}, u32[]{:S(2)}, u32[]{:S(2)}) collective-permute-start(f32[32,1,256]{2,0,1:T(8,128)S(1)} %get-tuple-element.37), channel_id=1, source_target_pairs={{16,0},{32,16},{48,32},{64,48},{80,64},{96,80},{112,96},{128,112},... | collective-permute-start | bytes 98312 | tf_op jit(solution)/shard_map/ppermute | solution.py:24
  271.6 10.7 %collective-permute-start.62 = (f32[3,2,260]{2,1,0:T(2,128)S(1)}, f32[3,2,260]{2,1,0:T(2,128)S(1)}, u32[]{:S(2)}, u32[]{:S(2)}) collective-permute-start(f32[3,2,260]{2,1,0:T(2,128)S(1)} %collective-permute-done.61), channel_id=1, source_target_pairs={{0,4},{1,5},{2,6},{3,7},{4,0},{5,1},{6,2},{7,3},{8,12},{9,13},{10,... | collective-permute-start | bytes 18728 | tf_op jit(solution)/shard_map/ppermute | solution.py:12
  282.3 9.5 %collective-permute-start.63 = (f32[3,2,260]{2,1,0:T(2,128)S(1)}, f32[3,2,260]{2,1,0:T(2,128)S(1)}, u32[]{:S(2)}, u32[]{:S(2)}) collective-permute-start(f32[3,2,260]{2,1,0:T(2,128)S(1)} %collective-permute-done.62), channel_id=1, source_target_pairs={{0,8},{1,9},{2,10},{3,11},{4,12},{5,13},{6,14},{7,15},{8,0},{9,1},... | collective-permute-start | bytes 18728 | tf_op jit(solution)/shard_map/ppermute | solution.py:12
  294.0 12.5 %collective-permute-start.64 = (f32[3,2,256]{2,1,0:T(2,128)}, f32[3,2,256]{2,1,0:T(2,128)S(1)}, u32[]{:S(2)}, u32[]{:S(2)}) collective-permute-start(f32[3,2,256]{2,1,0:T(2,128)} %get-tuple-element.147), channel_id=1, source_target_pairs={{0,16},{16,32},{32,48},{48,64},{64,80},{80,96},{96,112},{112,128},... | collective-permute-start | bytes 18440 | tf_op jit(solution)/shard_map/ppermute | solution.py:21
  295.9 10.6 %collective-permute-start.65 = (f32[3,2,256]{2,1,0:T(2,128)}, f32[3,2,256]{2,1,0:T(2,128)}, u32[]{:S(2)}, u32[]{:S(2)}) collective-permute-start(f32[3,2,256]{2,1,0:T(2,128)} %get-tuple-element.148), channel_id=1, source_target_pairs={{16,0},{32,16},{48,32},{64,48},{80,64},{96,80},{112,96},{128,112},... | collective-permute-start | bytes 18440 | tf_op jit(solution)/shard_map/ppermute | solution.py:24
  310.6 20.5 %collective-permute-start.4 = (f32[32,1,258]{2,0,1:T(8,128)}, f32[32,1,258]{2,0,1:T(8,128)}, u32[]{:S(2)}, u32[]{:S(2)}) collective-permute-start(f32[32,1,258]{2,0,1:T(8,128)} %broadcast_multiply_fusion), channel_id=1, source_target_pairs={{0,1},{1,0},{2,3},{3,2},{4,5},{5,4},{6,7},{7,6},{8,9},{9,8},{10,11... | collective-permute-start | bytes 99080 | tf_op jit(solution)/shard_map/ppermute | solution.py:12
  331.1 38.0 %collective-permute-start.5 = (f32[32,1,258]{2,0,1:T(8,128)}, f32[32,1,258]{2,0,1:T(8,128)}, u32[]{:S(2)}, u32[]{:S(2)}) collective-permute-start(f32[32,1,258]{2,0,1:T(8,128)} %collective-permute-done.4), channel_id=1, source_target_pairs={{0,2},{1,3},{2,0},{3,1},{4,6},{5,7},{6,4},{7,5},{8,10},{9,11},{10,... | collective-permute-start | bytes 99080 | tf_op jit(solution)/shard_map/ppermute | solution.py:12
  333.8 9.5 %collective-permute-start.71 = (f32[3,2,260]{2,1,0:T(2,128)S(1)}, f32[3,2,260]{2,1,0:T(2,128)S(1)}, u32[]{:S(2)}, u32[]{:S(2)}) collective-permute-start(f32[3,2,260]{2,1,0:T(2,128)S(1)} %collective-permute-done.70), channel_id=1, source_target_pairs={{0,8},{1,9},{2,10},{3,11},{4,12},{5,13},{6,14},{7,15},{8,0},{9,1},... | collective-permute-start | bytes 18728 | tf_op jit(solution)/shard_map/ppermute | solution.py:12
  359.0 14.3 %collective-permute-start.72 = (f32[3,2,256]{2,1,0:T(2,128)S(1)}, f32[3,2,256]{2,1,0:T(2,128)S(1)}, u32[]{:S(2)}, u32[]{:S(2)}) collective-permute-start(f32[3,2,256]{2,1,0:T(2,128)S(1)} %get-tuple-element.145), channel_id=1, source_target_pairs={{0,16},{16,32},{32,48},{48,64},{64,80},{80,96},{96,112},{112,128},... | collective-permute-start | bytes 18440 | tf_op jit(solution)/shard_map/ppermute | solution.py:21
  361.0 12.3 %collective-permute-start.73 = (f32[3,2,256]{2,1,0:T(2,128)S(1)}, f32[3,2,256]{2,1,0:T(2,128)S(1)}, u32[]{:S(2)}, u32[]{:S(2)}) collective-permute-start(f32[3,2,256]{2,1,0:T(2,128)S(1)} %get-tuple-element.146), channel_id=1, source_target_pairs={{16,0},{32,16},{48,32},{64,48},{80,64},{96,80},{112,96},{128,112},... | collective-permute-start | bytes 18440 | tf_op jit(solution)/shard_map/ppermute | solution.py:24
  377.7 10.7 %collective-permute-start.7 = (f32[32,1,258]{2,0,1:T(8,128)}, f32[32,1,258]{2,0,1:T(8,128)S(1)}, u32[]{:S(2)}, u32[]{:S(2)}) collective-permute-start(f32[32,1,258]{2,0,1:T(8,128)} %collective-permute-done.6), channel_id=1, source_target_pairs={{0,8},{1,9},{2,10},{3,11},{4,12},{5,13},{6,14},{7,15},{8,0},{9,1},... | collective-permute-start | bytes 99080 | tf_op jit(solution)/shard_map/ppermute | solution.py:12
  (76 other events, 601.6 us)
where the time goes:
time: 416 us; the launch traced here: 413 us
  starting transfers between devices  262 us (63%)
  waiting for transfers between devices  85.2 us (20%)
  local copies, waits for them, and re-layouts  32.2 us (8%)
  other arithmetic  30.7 us (7%)
    ppermute x40, starting transfers between devices, swapped(): return lax.ppermute(value, axis, pairs)  150 us
    ppermute x20, starting transfers between devices, extended_2(): lax.ppermute(lax.slice_in_dim(block, 0, width, axis=dim), axis, backward)  90.7 us
    ppermute x40, waiting for transfers between devices, swapped(): return lax.ppermute(value, axis, pairs)  68.7 us
    ppermute x20, starting transfers between devices, extended_2(): lax.ppermute(lax.slice_in_dim(block, block.shape[dim] - width, None, axis...  21.7 us
    unnamed x103, local copies, waits for them, and re-layouts  20.4 us
    ppermute x20, waiting for transfers between devices, extended_2(): lax.ppermute(lax.slice_in_dim(block, block.shape[dim] - width, None, axis...  10.1 us
  transfers between devices with their start and end apart: 80, of which 40 were waited for; matrix products, arithmetic and copies ran while one was open for 10% of the time, Pallas kernels for 0%

commit v1 on v0

v1 whole, which is shorter than its diff:
```python
import functools

import jax
import jax.numpy as jnp
from jax import lax
from jax.experimental import pallas as pl
from jax.experimental.pallas import tpu as pltpu
from jax.sharding import PartitionSpec as P

SUB = 8
HALO = 2 * SUB
MESH = pl.DeviceIdType.MESH

ST_N, ST_S, CF_N, CF_S = 0, 3, 6, 7
P_E, P_W, P_NE, P_SE, P_NW, P_SW = 8, 9, 10, 11, 12, 13
T_N, T_S, T_E, T_W = 14, 15, 16, 17
SLOTS = 18
UP_ST, DN_ST, UP_CF, DN_CF = 0, 3, 6, 7
SD_E, SD_W, SD_EU, SD_ED, SD_WU, SD_WD = 8, 9, 10, 11, 12, 13
SD_TU, SD_TD, SD_TE, SD_TW = 14, 15, 16, 17


def lanes(shape):
    return lax.broadcasted_iota(jnp.int32, shape, 1)


def flip_rows(tile):
    rows = tile.shape[0]
    index = 7 - lax.broadcasted_iota(jnp.int32, (8, 128), 0)
    parts = [
        jnp.take_along_axis(tile[r : r + 8], index, axis=0) for r in range(rows - 8, -8, -8)
    ]
    return jnp.concatenate(parts, axis=0)


def flip_lanes(tile, mask):
    index = lanes((8, 128)) ^ mask
    parts = [
        jnp.take_along_axis(tile[r : r + 8], index, axis=1) for r in range(0, tile.shape[0], 8)
    ]
    return jnp.concatenate(parts, axis=0)


def kernel(
    n_lat, n_lon,
    tr, th, mk, zu, mv, sf, zb, mb,
    o_tr, o_sf, o_zb, o_mb,
    t_v, h_v, m_v, u_v, v_v, w_v, c_v, out_v,
    x_v, y_v, a_v, pe, pw, re, rw, qe, qw, se, sw, gn, gs, hn, hs,
    load_sem, out_sem, send_sem, recv_sem,
):
    levels, rows, columns = t_v.shape
    wide = columns + 128
    top = HALO + rows
    lat, lon = lax.axis_index("lat"), lax.axis_index("lon")
    last, first = lat == n_lat - 1, lat == 0
    not_last, not_first = lat < n_lat - 1, lat > 0
    east, west = lax.rem(lon + 1, n_lon), lax.rem(lon + n_lon - 1, n_lon)
    mirror = n_lon - 1 - lon
    fold_e = lax.rem(2 * n_lon - 2 - lon, n_lon)
    fold_w = lax.rem(n_lon - lon, n_lon)
    self_e, self_w = fold_e == lon, fold_w == lon

    loads = [
        (th, h_v), (mk, m_v), (zu, u_v), (mv, v_v), (tr, t_v),
        (sf, x_v.at[0, pl.ds(HALO, rows), pl.ds(0, columns)]),
        (zb, x_v.at[1, pl.ds(HALO, rows), pl.ds(0, columns)]),
        (mb, x_v.at[2, pl.ds(HALO, rows), pl.ds(0, columns)]),
    ]
    loads = [pltpu.make_async_copy(s, d, load_sem.at[i]) for i, (s, d) in enumerate(loads)]
    for load in loads:
        load.start()

    barrier = pltpu.get_barrier_semaphore()

    def greet(to_lat, to_lon):
        pl.semaphore_signal(barrier, inc=1, device_id=(to_lat, to_lon), device_id_type=MESH)

    greet(lat, east)
    greet(lat, west)

    @pl.when(not_last)
    def _():
        greet(lat + 1, lon)
        greet(lat + 1, east)
        greet(lat + 1, west)

    @pl.when(not_first)
    def _():
        greet(lat - 1, lon)
        greet(lat - 1, east)
        greet(lat - 1, west)

    @pl.when(last)
    def _():
        greet(lat, mirror)

    @pl.when(last & jnp.logical_not(self_e))
    def _():
        greet(lat, fold_e)

    @pl.when(last & jnp.logical_not(self_w))
    def _():
        greet(lat, fold_w)

    def send(src, dst, out_slot, in_slot, to_lat, to_lon):
        return pltpu.make_async_remote_copy(
            src_ref=src, dst_ref=dst, send_sem=send_sem.at[out_slot],
            recv_sem=recv_sem.at[in_slot], device_id=(to_lat, to_lon), device_id_type=MESH,
        )

    def arrived(dst, in_slot):
        send(dst, dst, 0, in_slot, lat, east).wait_recv()

    def sent(src, out_slot):
        send(src, src, out_slot, 0, lat, east).wait_send()

    low, high = pl.ds(0, HALO), pl.ds(top, HALO)
    own_low, own_high = pl.ds(HALO, HALO), pl.ds(rows, HALO)
    all_columns = pl.ds(0, columns)
    state = (sf, zb, mb)

    def barrier_wait():
        ups = jnp.where(
            last, 1 + jnp.where(self_e, 0, 1) + jnp.where(self_w, 0, 1), 3
        )
        pl.semaphore_wait(barrier, 2 + ups + jnp.where(first, 0, 3))

    def send_state():
        for f in range(3):
            src = state[f].at[pl.ds(rows - HALO, HALO), :]

            @pl.when(not_last)
            def _():
                send(src, x_v.at[f, low, all_columns], UP_ST + f, ST_S + f, lat + 1, lon).start()

            @pl.when(last)
            def _():
                send(src, x_v.at[f, high, all_columns], UP_ST + f, ST_N + f, lat, mirror).start()

            @pl.when(not_first)
            def _():
                send(
                    state[f].at[low, :], x_v.at[f, high, all_columns],
                    DN_ST + f, ST_N + f, lat - 1, lon,
                ).start()

    def send_column():
        src = y_v.at[:, own_high, all_columns]

        @pl.when(not_last)
        def _():
            send(src, y_v.at[:, low, all_columns], UP_CF, CF_S, lat + 1, lon).start()

        @pl.when(last)
        def _():
            send(src, y_v.at[:, high, all_columns], UP_CF, CF_N, lat, mirror).start()

        @pl.when(not_first)
        def _():
            send(
                y_v.at[:, own_low, all_columns], y_v.at[:, high, all_columns],
                DN_CF, CF_N, lat - 1, lon,
            ).start()

    part_low, part_high = pl.ds(0, HALO), pl.ds(rows - HALO, HALO)
    middle = pl.ds(HALO, rows)

    def send_sides():
        send(pe, rw.at[middle], SD_E, P_W, lat, east).start()
        send(pw, re.at[middle], SD_W, P_E, lat, west).start()

        @pl.when(not_last)
        def _():
            send(pe.at[part_high], rw.at[low], SD_EU, P_SW, lat + 1, east).start()
            send(pw.at[part_high], re.at[low], SD_WU, P_SE, lat + 1, west).start()

        @pl.when(last & jnp.logical_not(self_e))
        def _():
            send(pe.at[part_high], re.at[high], SD_EU, P_NE, lat, fold_e).start()

        @pl.when(last & self_e)
        def _():
            pltpu.make_async_copy(pe.at[part_high], re.at[high], recv_sem.at[P_NE]).start()

        @pl.when(last & jnp.logical_not(self_w))
        def _():
            send(pw.at[part_high], rw.at[high], SD_WU, P_NW, lat, fold_w).start()

        @pl.when(last & self_w)
        def _():
            pltpu.make_async_copy(pw.at[part_high], rw.at[high], recv_sem.at[P_NW]).start()

        @pl.when(not_first)
        def _():
            send(pe.at[part_low], rw.at[high], SD_ED, P_NW, lat - 1, east).start()
            send(pw.at[part_low], re.at[high], SD_WD, P_NE, lat - 1, west).start()

    def send_tracer():
        @pl.when(not_last)
        def _():
            send(gn, hs, SD_TU, T_S, lat + 1, lon).start()

        @pl.when(last)
        def _():
            send(gn, hn, SD_TU, T_N, lat, mirror).start()

        @pl.when(not_first)
        def _():
            send(gs, hn, SD_TD, T_N, lat - 1, lon).start()

        send(qe, sw, SD_TE, T_W, lat, east).start()
        send(qw, se, SD_TW, T_E, lat, west).start()

    barrier_wait()
    send_state()

    for load in loads[:4]:
        load.wait()

    def add_level(k, sums):
        wet = m_v[k].astype(jnp.float32) * h_v[k]
        w_v[k] = wet
        return sums[0] + wet, sums[1] + wet * u_v[k], sums[2] + wet * v_v[k]

    zero = jnp.zeros((rows, columns), jnp.float32)
    depth, force_u, force_v = lax.fori_loop(0, levels, add_level, (zero, zero, zero))
    force_u, force_v = 0.05 * force_u, 0.05 * force_v
    y_v[0, pl.ds(HALO, rows), all_columns] = depth
    y_v[1, pl.ds(HALO, rows), all_columns] = force_u
    y_v[2, pl.ds(HALO, rows), all_columns] = force_v
    send_column()

    for load in loads[4:]:
        load.wait()

    lane = lanes((rows, 128))
    fields = [x_v[f, pl.ds(HALO, rows), all_columns] for f in range(3)] + [depth, force_u, force_v]
    pack_e = jnp.zeros((rows, 128), jnp.float32)
    pack_w = jnp.zeros((rows, 128), jnp.float32)
    for f in range(6):
        here = (lane >= HALO * f) & (lane < HALO * (f + 1))
        from_e = pltpu.roll(fields[f][:, columns - 128 :], (HALO * f + HALO) % 128, 1)
        pack_e = jnp.where(here, from_e, pack_e)
        from_w = fields[f][:, :128]
        if f:
            from_w = pltpu.roll(from_w, HALO * f, 1)
        pack_w = jnp.where(here, from_w, pack_w)
    pe[...] = pack_e
    pw[...] = pack_w
    send_sides()

    pack_e = jnp.zeros((rows, 128), jnp.float32)
    pack_w = jnp.zeros((rows, 128), jnp.float32)
    for i, source in enumerate((t_v, w_v, u_v)):
        for k in range(levels):
            slot = i * levels + k
            pack_e = jnp.where(
                lane == slot, pltpu.roll(source[k, :, columns - 128 :], slot + 1, 1), pack_e
            )
            from_w = source[k, :, :128]
            if slot:
                from_w = pltpu.roll(from_w, slot, 1)
            pack_w = jnp.where(lane == slot, from_w, pack_w)
    qe[...] = pack_e
    qw[...] = pack_w
    for i, source in enumerate((t_v, w_v, v_v)):
        gn[i] = source[:, rows - 1, :]
        gs[i] = source[:, 0, :]
    send_tracer()

    col = lanes((rows, columns))
    row = lax.broadcasted_iota(jnp.int32, (rows, columns), 0)

    def tracer_level(k, lower):
        t, w, u, v = t_v[k], w_v[k], u_v[k], v_v[k]
        t_e, w_e, u_e = (pltpu.roll(z, columns - 1, 1) for z in (t, w, u))
        flux = jnp.minimum(w, w_e) * (0.25 * (u + u_e) * (t + t_e) - 0.1 * (t_e - t))
        flux = jnp.where(col == columns - 1, 0.0, flux)
        flow = flux - pltpu.roll(flux, 1, 1)
        t_n, w_n, v_n = (pltpu.roll(z, rows - 1, 0) for z in (t, w, v))
        flux = jnp.minimum(w, w_n) * (0.25 * (v + v_n) * (t + t_n) - 0.1 * (t_n - t))
        flux = jnp.where(row == rows - 1, 0.0, flux)
        flow = flow + (flux - pltpu.roll(flux, 1, 0))
        above = jnp.minimum(k + 1, levels - 1)
        upper = 0.2 * jnp.minimum(w, w_v[above]) * (t_v[above] - t)
        scale = 0.2 * m_v[k].astype(jnp.float32) / h_v[k]
        c_v[k] = scale
        out_v[k] = t + scale * ((upper - lower) - flow)
        return upper

    lax.fori_loop(0, levels, tracer_level, zero)

    for f in range(3):
        arrived(x_v.at[f, high, all_columns], ST_N + f)
    arrived(y_v.at[:, high, all_columns], CF_N)
    arrived(re.at[middle], P_E)
    arrived(rw.at[middle], P_W)
    arrived(re.at[high], P_NE)
    arrived(rw.at[high], P_NW)

    @pl.when(not_first)
    def _():
        for f in range(3):
            arrived(x_v.at[f, low, all_columns], ST_S + f)
        arrived(y_v.at[:, low, all_columns], CF_S)
        arrived(re.at[low], P_SE)
        arrived(rw.at[low], P_SW)

    @pl.when(first)
    def _():
        for ref in (x_v, y_v):
            for f in range(3):
                ref[f, low, all_columns] = jnp.zeros((HALO, columns), jnp.float32)
        re[low] = jnp.zeros((HALO, 128), jnp.float32)
        rw[low] = jnp.zeros((HALO, 128), jnp.float32)

    @pl.when(last)
    def _():
        for ref in (x_v, y_v):
            for f in range(3):
                sign = 1.0 if f == 0 else -1.0
                old = ref[f, high, all_columns]
                tiles = [old[:, c : c + 128] for c in range(columns - 128, -128, -128)]
                new = jnp.concatenate([flip_lanes(flip_rows(t), 127) for t in tiles], axis=1)
                ref[f, high, all_columns] = sign * new
        field = lanes((HALO, 128)) // HALO
        even = (field == 0) | (field == 3)
        for ref in (re, rw):
            new = flip_lanes(flip_rows(ref[high]), HALO - 1)
            ref[high] = jnp.where(even, new, -new)

    ext = x_v.shape[1]
    lane = lanes((ext, 128))
    from_e, from_w = re[...], rw[...]
    for f in range(6):
        shift = (128 - HALO * f) % 128
        tile_e = pltpu.roll(from_e, shift, 1) if shift else from_e
        shift = 128 - HALO - HALO * f
        tile_w = pltpu.roll(from_w, shift, 1) if shift else from_w
        ref = x_v if f < 3 else y_v
        ref[f % 3, :, pl.ds(columns, 128)] = jnp.where(lane < 64, tile_e, tile_w)

    d = y_v[0]
    a_v[0] = jnp.minimum(2.0 * d, 1.0)
    a_v[1] = 0.5 * jnp.minimum(d, pltpu.roll(d, wide - 1, 1))
    a_v[2] = 0.5 * jnp.minimum(d, pltpu.roll(d, ext - 1, 0))
    a_v[3] = 0.2 * y_v[1]
    a_v[4] = 0.2 * y_v[2]

    def cycles(span):
        count = span.size

        def step(_, carry):
            eta, ub, vb = (x_v[f, span, :] for f in range(3))
            wet = a_v[0, span, :]
            flux = a_v[1, span, :] * (ub + pltpu.roll(ub, wide - 1, 1))
            div = flux - pltpu.roll(flux, 1, 1)
            flux = a_v[2, span, :] * (vb + pltpu.roll(vb, count - 1, 0))
            div = div + (flux - pltpu.roll(flux, 1, 0))
            eta = eta - 0.2 * wet * div
            slope_x = pltpu.roll(eta, wide - 1, 1) - pltpu.roll(eta, 1, 1)
            slope_y = pltpu.roll(eta, count - 1, 0) - pltpu.roll(eta, 1, 0)
            x_v[0, span, :] = eta
            x_v[1, span, :] = wet * (ub - 0.05 * slope_x + a_v[3, span, :])
            x_v[2, span, :] = wet * (vb - 0.05 * slope_y + a_v[4, span, :])
            return carry

        lax.fori_loop(0, SUB // 2, step, 0)

    cycles(pl.ds(0, ext))
    cycles(pl.ds(SUB, ext - HALO))

    outs = [
        pltpu.make_async_copy(
            x_v.at[f, pl.ds(HALO, rows), all_columns], (o_sf, o_zb, o_mb)[f], out_sem.at[f]
        )
        for f in range(3)
    ]
    for out in outs:
        out.start()

    arrived(hn, T_N)
    arrived(se, T_E)
    arrived(sw, T_W)

    @pl.when(not_first)
    def _():
        arrived(hs, T_S)

    @pl.when(first)
    def _():
        hs[...] = jnp.zeros(hs.shape, jnp.float32)

    @pl.when(last)
    def _():
        for i in range(3):
            sign = -1.0 if i == 2 else 1.0
            old = hn[i]
            tiles = [old[:, c : c + 128] for c in range(columns - 128, -128, -128)]
            hn[i] = sign * jnp.concatenate([flip_lanes(t, 127) for t in tiles], axis=1)

    def face(t_a, t_b, w_a, w_b, u_a, u_b):
        return jnp.minimum(w_a, w_b) * (0.25 * (u_a + u_b) * (t_a + t_b) - 0.1 * (t_b - t_a))

    def packed_face(a, b):
        a_1, b_1 = pltpu.roll(a, 128 - levels, 1), pltpu.roll(b, 128 - levels, 1)
        a_2, b_2 = pltpu.roll(a, 128 - 2 * levels, 1), pltpu.roll(b, 128 - 2 * levels, 1)
        return face(a, b, a_1, b_1, a_2, b_2)

    flux_e = packed_face(qe[...], se[...])
    flux_w = packed_face(sw[...], qw[...])
    lane = lanes((rows, 128))
    for k in range(levels):
        edge = pl.ds(columns - 128, 128)
        moved = pltpu.roll(flux_e, 127 - k, 1)
        out_v[k, :, edge] = out_v[k, :, edge] - jnp.where(
            lane == 127, c_v[k, :, edge] * moved, 0.0
        )
        edge = pl.ds(0, 128)
        moved = pltpu.roll(flux_w, 128 - k, 1) if k else flux_w
        out_v[k, :, edge] = out_v[k, :, edge] + jnp.where(lane == 0, c_v[k, :, edge] * moved, 0.0)
    flux_n = face(gn[0], hn[0], gn[1], hn[1], gn[2], hn[2])
    out_v[:, rows - 1, :] = out_v[:, rows - 1, :] - c_v[:, rows - 1, :] * flux_n
    flux_s = face(hs[0], gs[0], hs[1], gs[1], hs[2], gs[2])
    out_v[:, 0, :] = out_v[:, 0, :] + c_v[:, 0, :] * flux_s

    out = pltpu.make_async_copy(out_v, o_tr, out_sem.at[3])
    out.start()

    for f in range(3):
        sent(state[f].at[low, :], UP_ST + f)
    sent(y_v.at[:, low, all_columns], UP_CF)
    sent(pe, SD_E)
    sent(pw, SD_W)
    sent(gn, SD_TU)
    sent(qe, SD_TE)
    sent(qw, SD_TW)

    @pl.when(not_last | jnp.logical_not(self_e))
    def _():
        sent(pe.at[part_high], SD_EU)

    @pl.when(not_last | jnp.logical_not(self_w))
    def _():
        sent(pw.at[part_high], SD_WU)

    @pl.when(not_first)
    def _():
        for f in range(3):
            sent(state[f].at[low, :], DN_ST + f)
        sent(y_v.at[:, low, all_columns], DN_CF)
        sent(pe.at[part_low], SD_ED)
        sent(pw.at[part_low], SD_WD)
        sent(gs, SD_TD)

    for copy in outs:
        copy.wait()
    out.wait()


def on_device(n_lat, n_lon, *args):
    levels, rows, columns = args[0].shape
    block = pltpu.VMEM((levels, rows, columns), jnp.float32)
    ext, wide = rows + 2 * HALO, columns + 128
    strip, long_strip = pltpu.VMEM((rows, 128), jnp.float32), pltpu.VMEM((ext, 128), jnp.float32)
    line = pltpu.VMEM((3, levels, columns), jnp.float32)
    flat = pltpu.VMEM((3, ext, wide), jnp.float32)
    scratch = [block, block, pltpu.VMEM((levels, rows, columns), jnp.int32)] + [block] * 5
    scratch += [flat] * 2 + [pltpu.VMEM((5, ext, wide), jnp.float32)] + [strip] * 2 + [long_strip] * 2 + [strip] * 4 + [line] * 4
    scratch += [
        pltpu.SemaphoreType.DMA((8,)), pltpu.SemaphoreType.DMA((4,)),
        pltpu.SemaphoreType.DMA((SLOTS,)), pltpu.SemaphoreType.DMA((SLOTS,)),
    ]
    whole = jax.ShapeDtypeStruct((levels, rows, columns), jnp.float32)
    surface = jax.ShapeDtypeStruct((rows, columns), jnp.float32)
    return pl.pallas_call(
        functools.partial(kernel, n_lat, n_lon),
        out_shape=(whole, surface, surface, surface),
        in_specs=[pl.BlockSpec(memory_space=pl.ANY)] * 8,
        out_specs=(pl.BlockSpec(memory_space=pl.ANY),) * 4,
        scratch_shapes=scratch,
        compiler_params=pltpu.CompilerParams(collective_id=0, has_side_effects=True),
        name="ocean",
    )(*args)


def solution(mesh):
    whole, surface = P(None, "lat", "lon"), P("lat", "lon")
    return jax.shard_map(
        functools.partial(on_device, mesh.shape["lat"], mesh.shape["lon"]),
        mesh=mesh,
        in_specs=(whole,) * 5 + (surface,) * 3,
        out_specs=(whole, surface, surface, surface),
        check_vma=False,
    )
```

time: 416 us -> 27.3 us (0.07)
  the two profiles are of different devices: /device:TPU:64 before, /device:TPU:63 now
where the time goes in v1:
time: 27.3 us; the launch traced here: 27 us
  Pallas kernels  22.6 us (83%)
  local copies, waits for them, and re-layouts  3.83 us (14%)
  between operations  0.65 us (2%)
    pallas_call x1, Pallas kernels, on_device(): pl.pallas_call(functools.partial(kernel, n_lat, n_lon), out_shape=(whole,...  22.6 us
    unnamed x10, local copies, waits for them, and re-layouts  3.83 us

profile of v1, /device:TPU:63, one launch (start us, length us, event | category | flops | bytes accessed | tf_op | source)
XLA Modules:
  0.0 27.0 jit_solution(18322614615731365632)
XLA Ops:
  0.6 22.6 %ocean.1 = (f32[8,32,256]{2,1,0:T(8,128)}, f32[32,256]{1,0:T(8,128)}, f32[32,256]{1,0:T(8,128)}, f32[32,256]{1,0:T(8,128)}) custom-call(f32[8,32,256]{2,1,0:T(8,128)} %tr.1, f32[8,32,256]{2,1,0:T(8,128)} %th.1, s32[8,32,256]{2,1,0:T(8,128)} %mk.1, f32[8,32,256]{2,1,0:T(8,128)} %zu.1, f32[8,32,256]{2,1,0:T(8,128)} %mv.1, f32[32,256]{1,0:T(8,128)} %sf.1, ...), custom_call_target="tpu_custom_call" | custom-call | tf_op jit(solution)/shard_map/ocean/pallas_call | solution.py:477
  23.2 0.0 copy-start.2
  23.2 1.7 %copy.16 = f32[8,32,256]{2,1,0:T(8,128)} copy(f32[8,32,256]{2,1,0:T(8,128)} %get-tuple-element.8) | data formatting | bytes 524288
  24.9 0.0 copy-done.2
  24.9 0.0 copy-start.1
  24.9 0.6 %copy.17 = f32[32,256]{1,0:T(8,128)} copy(f32[32,256]{1,0:T(8,128)S(1)} %copy-done.2) | data formatting | bytes 65536
  25.5 0.2 copy-done.1
  25.7 0.0 copy-start
  25.7 0.6 %copy.18 = f32[32,256]{1,0:T(8,128)} copy(f32[32,256]{1,0:T(8,128)S(1)} %copy-done.1) | data formatting | bytes 65536
  26.3 0.2 copy-done
  26.4 0.6 %copy.19 = f32[32,256]{1,0:T(8,128)} copy(f32[32,256]{1,0:T(8,128)S(1)} %copy-done) | data formatting | bytes 65536
Async XLA Ops:
  23.2 1.7 %copy-start.2 = (f32[32,256]{1,0:T(8,128)S(1)}, f32[32,256]{1,0:T(8,128)}, u32[]{:S(2)}) copy-start(f32[32,256]{1,0:T(8,128)} %get-tuple-element.9) | copy-start | bytes 98308
  24.9 0.8 %copy-start.1 = (f32[32,256]{1,0:T(8,128)S(1)}, f32[32,256]{1,0:T(8,128)}, u32[]{:S(2)}) copy-start(f32[32,256]{1,0:T(8,128)} %get-tuple-element.10) | copy-start | bytes 98308
  25.7 0.8 %copy-start = (f32[32,256]{1,0:T(8,128)S(1)}, f32[32,256]{1,0:T(8,128)}, u32[]{:S(2)}) copy-start(f32[32,256]{1,0:T(8,128)} %get-tuple-element.11) | copy-start | bytes 98308

commit v2 on v1

--- a/solution.py
+++ b/solution.py
@@ -11,13 +11,9 @@
 HALO = 2 * SUB
 MESH = pl.DeviceIdType.MESH
 
-ST_N, ST_S, CF_N, CF_S = 0, 3, 6, 7
-P_E, P_W, P_NE, P_SE, P_NW, P_SW = 8, 9, 10, 11, 12, 13
-T_N, T_S, T_E, T_W = 14, 15, 16, 17
-SLOTS = 18
-UP_ST, DN_ST, UP_CF, DN_CF = 0, 3, 6, 7
-SD_E, SD_W, SD_EU, SD_ED, SD_WU, SD_WD = 8, 9, 10, 11, 12, 13
-SD_TU, SD_TD, SD_TE, SD_TW = 14, 15, 16, 17
+F_N, F_S, P_E, P_W, P_NE, P_SE, P_NW, P_SW, T_N, T_S, T_E, T_W = range(12)
+UP_F, DN_F, SD_E, SD_W, SD_EU, SD_ED, SD_WU, SD_WD, SD_TU, SD_TD, SD_TE, SD_TW = range(12)
+SLOTS = 12
 
 
 def lanes(shape):
@@ -44,10 +40,10 @@
 def kernel(
     n_lat, n_lon,
     tr, th, mk, zu, mv, sf, zb, mb,
-    o_tr, o_sf, o_zb, o_mb,
-    t_v, h_v, m_v, u_v, v_v, w_v, c_v, out_v,
-    x_v, y_v, a_v, pe, pw, re, rw, qe, qw, se, sw, gn, gs, hn, hs,
-    load_sem, out_sem, send_sem, recv_sem,
+    out_v, o_st,
+    t_v, h_v, m_v, u_v, v_v, w_v, c_v,
+    f_v, a_v, pe, pw, re, rw, qe, qw, se, sw, gn, gs, hn, hs,
+    load_sem, send_sem, recv_sem,
 ):
     levels, rows, columns = t_v.shape
     wide = columns + 128
@@ -61,15 +57,18 @@
     fold_w = lax.rem(n_lon - lon, n_lon)
     self_e, self_w = fold_e == lon, fold_w == lon
 
+    low, middle, high = pl.ds(0, HALO), pl.ds(HALO, rows), pl.ds(top, HALO)
+    own_low, own_high = pl.ds(HALO, HALO), pl.ds(rows, HALO)
+    part_low, part_high = pl.ds(0, HALO), pl.ds(rows - HALO, HALO)
+    all_columns = pl.ds(0, columns)
+
     loads = [
         (th, h_v), (mk, m_v), (zu, u_v), (mv, v_v), (tr, t_v),
-        (sf, x_v.at[0, pl.ds(HALO, rows), pl.ds(0, columns)]),
-        (zb, x_v.at[1, pl.ds(HALO, rows), pl.ds(0, columns)]),
-        (mb, x_v.at[2, pl.ds(HALO, rows), pl.ds(0, columns)]),
+        (sf, f_v.at[0, middle, all_columns]),
+        (zb, f_v.at[1, middle, all_columns]),
+        (mb, f_v.at[2, middle, all_columns]),
     ]
     loads = [pltpu.make_async_copy(s, d, load_sem.at[i]) for i, (s, d) in enumerate(loads)]
-    for load in loads:
-        load.start()
 
     barrier = pltpu.get_barrier_semaphore()
 
@@ -102,6 +101,9 @@
     @pl.when(last & jnp.logical_not(self_w))
     def _():
         greet(lat, fold_w)
+
+    for load in loads:
+        load.start()
 
     def send(src, dst, out_slot, in_slot, to_lat, to_lon):
         return pltpu.make_async_remote_copy(
@@ -115,10 +117,6 @@
     def sent(src, out_slot):
         send(src, src, out_slot, 0, lat, east).wait_send()
 
-    low, high = pl.ds(0, HALO), pl.ds(top, HALO)
-    own_low, own_high = pl.ds(HALO, HALO), pl.ds(rows, HALO)
-    all_columns = pl.ds(0, columns)
-    state = (sf, zb, mb)
 
     def barrier_wait():
         ups = jnp.where(
@@ -126,45 +124,23 @@
         )
         pl.semaphore_wait(barrier, 2 + ups + jnp.where(first, 0, 3))
 
-    def send_state():
-        for f in range(3):
-            src = state[f].at[pl.ds(rows - HALO, HALO), :]
-
-            @pl.when(not_last)
-            def _():
-                send(src, x_v.at[f, low, all_columns], UP_ST + f, ST_S + f, lat + 1, lon).start()
-
-            @pl.when(last)
-            def _():
-                send(src, x_v.at[f, high, all_columns], UP_ST + f, ST_N + f, lat, mirror).start()
-
-            @pl.when(not_first)
-            def _():
-                send(
-                    state[f].at[low, :], x_v.at[f, high, all_columns],
-                    DN_ST + f, ST_N + f, lat - 1, lon,
-                ).start()
-
-    def send_column():
-        src = y_v.at[:, own_high, all_columns]
+    def send_fields():
+        src = f_v.at[:, own_high, all_columns]
 
         @pl.when(not_last)
         def _():
-            send(src, y_v.at[:, low, all_columns], UP_CF, CF_S, lat + 1, lon).start()
+            send(src, f_v.at[:, low, all_columns], UP_F, F_S, lat + 1, lon).start()
 
         @pl.when(last)
         def _():
-            send(src, y_v.at[:, high, all_columns], UP_CF, CF_N, lat, mirror).start()
+            send(src, f_v.at[:, high, all_columns], UP_F, F_N, lat, mirror).start()
 
         @pl.when(not_first)
         def _():
             send(
-                y_v.at[:, own_low, all_columns], y_v.at[:, high, all_columns],
-                DN_CF, CF_N, lat - 1, lon,
+                f_v.at[:, own_low, all_columns], f_v.at[:, high, all_columns],
+                DN_F, F_N, lat - 1, lon,
             ).start()
-
-    part_low, part_high = pl.ds(0, HALO), pl.ds(rows - HALO, HALO)
-    middle = pl.ds(HALO, rows)
 
     def send_sides():
         send(pe, rw.at[middle], SD_E, P_W, lat, east).start()
@@ -211,9 +187,6 @@
 
         send(qe, sw, SD_TE, T_W, lat, east).start()
         send(qw, se, SD_TW, T_E, lat, west).start()
-
-    barrier_wait()
-    send_state()
 
     for load in loads[:4]:
         load.wait()
@@ -226,16 +199,15 @@
     zero = jnp.zeros((rows, columns), jnp.float32)
     depth, force_u, force_v = lax.fori_loop(0, levels, add_level, (zero, zero, zero))
     force_u, force_v = 0.05 * force_u, 0.05 * force_v
-    y_v[0, pl.ds(HALO, rows), all_columns] = depth
-    y_v[1, pl.ds(HALO, rows), all_columns] = force_u
-    y_v[2, pl.ds(HALO, rows), all_columns] = force_v
-    send_column()
+    f_v[3, middle, all_columns] = depth
+    f_v[4, middle, all_columns] = force_u
+    f_v[5, middle, all_columns] = force_v
 
     for load in loads[4:]:
         load.wait()
 
     lane = lanes((rows, 128))
-    fields = [x_v[f, pl.ds(HALO, rows), all_columns] for f in range(3)] + [depth, force_u, force_v]
+    fields = [f_v[f, middle, all_columns] for f in range(3)] + [depth, force_u, force_v]
     pack_e = jnp.zeros((rows, 128), jnp.float32)
     pack_w = jnp.zeros((rows, 128), jnp.float32)
     for f in range(6):
@@ -248,7 +220,9 @@
         pack_w = jnp.where(here, from_w, pack_w)
     pe[...] = pack_e
     pw[...] = pack_w
+    barrier_wait()
     send_sides()
+    send_fields()
 
     pack_e = jnp.zeros((rows, 128), jnp.float32)
     pack_w = jnp.zeros((rows, 128), jnp.float32)
@@ -291,9 +265,7 @@
 
     lax.fori_loop(0, levels, tracer_level, zero)
 
-    for f in range(3):
-        arrived(x_v.at[f, high, all_columns], ST_N + f)
-    arrived(y_v.at[:, high, all_columns], CF_N)
+    arrived(f_v.at[:, high, all_columns], F_N)
     arrived(re.at[middle], P_E)
     arrived(rw.at[middle], P_W)
     arrived(re.at[high], P_NE)
@@ -301,36 +273,30 @@
 
     @pl.when(not_first)
     def _():
-        for f in range(3):
-            arrived(x_v.at[f, low, all_columns], ST_S + f)
-        arrived(y_v.at[:, low, all_columns], CF_S)
+        arrived(f_v.at[:, low, all_columns], F_S)
         arrived(re.at[low], P_SE)
         arrived(rw.at[low], P_SW)
 
     @pl.when(first)
     def _():
-        for ref in (x_v, y_v):
-            for f in range(3):
-                ref[f, low, all_columns] = jnp.zeros((HALO, columns), jnp.float32)
+        f_v[:, low, all_columns] = jnp.zeros((6, HALO, columns), jnp.float32)
         re[low] = jnp.zeros((HALO, 128), jnp.float32)
         rw[low] = jnp.zeros((HALO, 128), jnp.float32)
 
     @pl.when(last)
     def _():
-        for ref in (x_v, y_v):
-            for f in range(3):
-                sign = 1.0 if f == 0 else -1.0
-                old = ref[f, high, all_columns]
-                tiles = [old[:, c : c + 128] for c in range(columns - 128, -128, -128)]
-                new = jnp.concatenate([flip_lanes(flip_rows(t), 127) for t in tiles], axis=1)
-                ref[f, high, all_columns] = sign * new
+        for f in range(6):
+            old = f_v[f, high, all_columns]
+            tiles = [old[:, c : c + 128] for c in range(columns - 128, -128, -128)]
+            new = jnp.concatenate([flip_lanes(flip_rows(t), 127) for t in tiles], axis=1)
+            f_v[f, high, all_columns] = new if f % 3 == 0 else -new
         field = lanes((HALO, 128)) // HALO
         even = (field == 0) | (field == 3)
         for ref in (re, rw):
             new = flip_lanes(flip_rows(ref[high]), HALO - 1)
             ref[high] = jnp.where(even, new, -new)
 
-    ext = x_v.shape[1]
+    ext = f_v.shape[1]
     lane = lanes((ext, 128))
     from_e, from_w = re[...], rw[...]
     for f in range(6):
@@ -338,21 +304,26 @@
         tile_e = pltpu.roll(from_e, shift, 1) if shift else from_e
         shift = 128 - HALO - HALO * f
         tile_w = pltpu.roll(from_w, shift, 1) if shift else from_w
-        ref = x_v if f < 3 else y_v
-        ref[f % 3, :, pl.ds(columns, 128)] = jnp.where(lane < 64, tile_e, tile_w)
-
-    d = y_v[0]
+        f_v[f, :, pl.ds(columns, 128)] = jnp.where(lane < 64, tile_e, tile_w)
+
+    sent(f_v.at[:, own_high, all_columns], UP_F)
+
+    @pl.when(not_first)
+    def _():
+        sent(f_v.at[:, own_low, all_columns], DN_F)
+
+    d = f_v[3]
     a_v[0] = jnp.minimum(2.0 * d, 1.0)
     a_v[1] = 0.5 * jnp.minimum(d, pltpu.roll(d, wide - 1, 1))
     a_v[2] = 0.5 * jnp.minimum(d, pltpu.roll(d, ext - 1, 0))
-    a_v[3] = 0.2 * y_v[1]
-    a_v[4] = 0.2 * y_v[2]
+    a_v[3] = 0.2 * f_v[4]
+    a_v[4] = 0.2 * f_v[5]
 
     def cycles(span):
         count = span.size
 
         def step(_, carry):
-            eta, ub, vb = (x_v[f, span, :] for f in range(3))
+            eta, ub, vb = (f_v[f, span, :] for f in range(3))
             wet = a_v[0, span, :]
             flux = a_v[1, span, :] * (ub + pltpu.roll(ub, wide - 1, 1))
             div = flux - pltpu.roll(flux, 1, 1)
@@ -361,9 +332,9 @@
             eta = eta - 0.2 * wet * div
             slope_x = pltpu.roll(eta, wide - 1, 1) - pltpu.roll(eta, 1, 1)
             slope_y = pltpu.roll(eta, count - 1, 0) - pltpu.roll(eta, 1, 0)
-            x_v[0, span, :] = eta
-            x_v[1, span, :] = wet * (ub - 0.05 * slope_x + a_v[3, span, :])
-            x_v[2, span, :] = wet * (vb - 0.05 * slope_y + a_v[4, span, :])
+            f_v[0, span, :] = eta
+            f_v[1, span, :] = wet * (ub - 0.05 * slope_x + a_v[3, span, :])
+            f_v[2, span, :] = wet * (vb - 0.05 * slope_y + a_v[4, span, :])
             return carry
 
         lax.fori_loop(0, SUB // 2, step, 0)
@@ -371,14 +342,8 @@
     cycles(pl.ds(0, ext))
     cycles(pl.ds(SUB, ext - HALO))
 
-    outs = [
-        pltpu.make_async_copy(
-            x_v.at[f, pl.ds(HALO, rows), all_columns], (o_sf, o_zb, o_mb)[f], out_sem.at[f]
-        )
-        for f in range(3)
-    ]
-    for out in outs:
-        out.start()
+    for f in range(3):
+        o_st[f] = f_v[f, middle, all_columns]
 
     arrived(hn, T_N)
     arrived(se, T_E)
@@ -425,12 +390,6 @@
     flux_s = face(hs[0], gs[0], hs[1], gs[1], hs[2], gs[2])
     out_v[:, 0, :] = out_v[:, 0, :] + c_v[:, 0, :] * flux_s
 
-    out = pltpu.make_async_copy(out_v, o_tr, out_sem.at[3])
-    out.start()
-
-    for f in range(3):
-        sent(state[f].at[low, :], UP_ST + f)
-    sent(y_v.at[:, low, all_columns], UP_CF)
     sent(pe, SD_E)
     sent(pw, SD_W)
     sent(gn, SD_TU)
@@ -447,16 +406,19 @@
 
     @pl.when(not_first)
     def _():
-        for f in range(3):
-            sent(state[f].at[low, :], DN_ST + f)
-        sent(y_v.at[:, low, all_columns], DN_CF)
         sent(pe.at[part_low], SD_ED)
         sent(pw.at[part_low], SD_WD)
         sent(gs, SD_TD)
 
-    for copy in outs:
+
+def store_kernel(tr, st, o_tr, o_sf, o_zb, o_mb, sem):
+    copies = [pltpu.make_async_copy(tr, o_tr, sem.at[3])]
+    for f, dst in enumerate((o_sf, o_zb, o_mb)):
+        copies.append(pltpu.make_async_copy(st.at[f], dst, sem.at[f]))
+    for copy in copies:
+        copy.start()
+    for copy in copies:
         copy.wait()
-    out.wait()
 
 
 def on_device(n_lat, n_lon, *args):
@@ -465,24 +427,40 @@
     ext, wide = rows + 2 * HALO, columns + 128
     strip, long_strip = pltpu.VMEM((rows, 128), jnp.float32), pltpu.VMEM((ext, 128), jnp.float32)
     line = pltpu.VMEM((3, levels, columns), jnp.float32)
-    flat = pltpu.VMEM((3, ext, wide), jnp.float32)
-    scratch = [block, block, pltpu.VMEM((levels, rows, columns), jnp.int32)] + [block] * 5
-    scratch += [flat] * 2 + [pltpu.VMEM((5, ext, wide), jnp.float32)] + [strip] * 2 + [long_strip] * 2 + [strip] * 4 + [line] * 4
+    flat = pltpu.VMEM((6, ext, wide), jnp.float32)
+    scratch = [block, block, pltpu.VMEM((levels, rows, columns), jnp.int32)] + [block] * 4
+    scratch += [flat] + [pltpu.VMEM((5, ext, wide), jnp.float32)]
+    scratch += [strip] * 2 + [long_strip] * 2 + [strip] * 4 + [line] * 4
     scratch += [
-        pltpu.SemaphoreType.DMA((8,)), pltpu.SemaphoreType.DMA((4,)),
+        pltpu.SemaphoreType.DMA((8,)),
         pltpu.SemaphoreType.DMA((SLOTS,)), pltpu.SemaphoreType.DMA((SLOTS,)),
     ]
     whole = jax.ShapeDtypeStruct((levels, rows, columns), jnp.float32)
     surface = jax.ShapeDtypeStruct((rows, columns), jnp.float32)
-    return pl.pallas_call(
+    in_vmem = pl.BlockSpec(memory_space=pltpu.VMEM)
+    anywhere = pl.BlockSpec(memory_space=pl.ANY)
+    args = [pltpu.with_memory_space_constraint(a, pltpu.HBM) for a in args]
+    tracer, state = pl.pallas_call(
         functools.partial(kernel, n_lat, n_lon),
-        out_shape=(whole, surface, surface, surface),
-        in_specs=[pl.BlockSpec(memory_space=pl.ANY)] * 8,
-        out_specs=(pl.BlockSpec(memory_space=pl.ANY),) * 4,
+        out_shape=(whole, jax.ShapeDtypeStruct((3, rows, columns), jnp.float32)),
+        in_specs=[anywhere] * 8,
+        out_specs=(in_vmem,) * 2,
         scratch_shapes=scratch,
-        compiler_params=pltpu.CompilerParams(collective_id=0, has_side_effects=True),
+        compiler_params=pltpu.CompilerParams(
+            collective_id=0, has_side_effects=True, vmem_limit_bytes=32 << 20
+        ),
         name="ocean",
     )(*args)
+    return pl.pallas_call(
+        store_kernel,
+        out_shape=(whole, surface, surface, surface),
+        in_specs=[in_vmem] * 2,
+        out_specs=(anywhere,) * 4,
+        scratch_shapes=[pltpu.SemaphoreType.DMA((4,))],
+        compiler_params=pltpu.CompilerParams(vmem_limit_bytes=32 << 20),
+
+        name="store",
+    )(tracer, state)
 
 
 def solution(mesh):

time: 27.3 us -> 23.4 us (0.86)
  local copies, waits for them, and re-layouts: 3.83 us -> 0 us
    unnamed x10 -> x0, local copies, waits for them, and re-layouts: 3.83 us -> none
    pallas_call x0 -> x1, Pallas kernels: none -> 0.76 us  [on_device(): pl.pallas_call(store_kernel, out_shape=(whole, surface, surface, surface)...]
    pallas_call x1, Pallas kernels: 22.6 us -> 21.9 us  [on_device(): pl.pallas_call(functools.partial(kernel, n_lat, n_lon), out_shape=(whole,...]
where the time goes in v2:
time: 23.4 us; the launch traced here: 23.3 us
  Pallas kernels  22.6 us (97%)
  between operations  0.64 us (3%)
    pallas_call x1, Pallas kernels, on_device(): pl.pallas_call(functools.partial(kernel, n_lat, n_lon), out_shape=(whole,...  21.9 us
    pallas_call x1, Pallas kernels, on_device(): pl.pallas_call(store_kernel, out_shape=(whole, surface, surface, surface)...  0.76 us

profile of v2, /device:TPU:63, one launch (start us, length us, event | category | flops | bytes accessed | tf_op | source)
XLA Modules:
  0.0 23.3 jit_solution(3967020272016230170)
XLA Ops:
  0.6 21.9 %ocean.1 = (f32[8,32,256]{2,1,0:T(8,128)S(1)}, f32[3,32,256]{2,1,0:T(8,128)S(1)}) custom-call(f32[8,32,256]{2,1,0:T(8,128)} %tr.1, f32[8,32,256]{2,1,0:T(8,128)} %th.1, s32[8,32,256]{2,1,0:T(8,128)} %mk.1, f32[8,32,256]{2,1,0:T(8,128)} %zu.1, f32[8,32,256]{2,1,0:T(8,128)} %mv.1, f32[32,256]{1,0:T(8,128)} %sf.1, f32[32,256]{1,0:T(8,128)} %zb.1, f32[32,256]{1,0:T(8,128)} %mb.1), custom_call_target="tpu_custom_call" | custom-call | tf_op jit(solution)/shard_map/ocean/pallas_call | solution.py:443
  22.5 0.8 %store.1 = (f32[8,32,256]{2,1,0:T(8,128)}, f32[32,256]{1,0:T(8,128)}, f32[32,256]{1,0:T(8,128)}, f32[32,256]{1,0:T(8,128)}) custom-call(f32[8,32,256]{2,1,0:T(8,128)S(1)} %get-tuple-element.6.tr, f32[3,32,256]{2,1,0:T(8,128)S(1)} %get-tuple-element.7.st), custom_call_target="tpu_custom_call" | custom-call | tf_op jit(solution)/shard_map/store/pallas_call | solution.py:454

commit v3 on v2

v3 whole, which is shorter than its diff:
```python
import functools

import jax
import jax.numpy as jnp
from jax import lax
from jax.experimental import pallas as pl
from jax.experimental.pallas import tpu as pltpu
from jax.sharding import PartitionSpec as P

SUB = 8
HALO = 2 * SUB
RING = 8
PAD = 8
CHUNK = 8
MESH = pl.DeviceIdType.MESH

ST_N, ST_S, CF_N, CF_S = 0, 6, 12, 13
P_E, P_W, P_NE, P_SE, P_NW, P_SW = 14, 15, 16, 17, 18, 19
T_N, T_S, T_E, T_W = 20, 21, 22, 23
UP_ST, DN_ST, UP_CF, DN_CF = 0, 6, 12, 13
SD_E, SD_W, SD_EU, SD_ED, SD_WU, SD_WD = 14, 15, 16, 17, 18, 19
SD_TU, SD_TD, SD_TE, SD_TW = 20, 21, 22, 23
SLOTS = 24
N, S, E, W, NE, NW, SE, SW, FOLD, FOLD_E, FOLD_W = range(11)
OPPOSITE = (S, N, W, E, SW, SE, NW, NE, FOLD, FOLD_E, FOLD_W)


def lanes(shape):
    return lax.broadcasted_iota(jnp.int32, shape, 1)


def flip_rows(tile):
    rows = tile.shape[0]
    index = 7 - lax.broadcasted_iota(jnp.int32, (8, 128), 0)
    parts = [
        jnp.take_along_axis(tile[r : r + 8], index, axis=0) for r in range(rows - 8, -8, -8)
    ]
    return jnp.concatenate(parts, axis=0)


def flip_lanes(tile, mask):
    index = lanes((8, 128)) ^ mask
    parts = [
        jnp.take_along_axis(tile[r : r + 8], index, axis=1) for r in range(0, tile.shape[0], 8)
    ]
    return jnp.concatenate(parts, axis=0)


def kernel(
    n_lat, n_lon,
    tr, th, mk, zu, mv, sf, zb, mb,
    out_v, o_st,
    t_v, h_v, m_v, u_v, v_v, w_v, c_v,
    x_0, x_1, x_2, f_v, a_v, pe, pw, re, rw, qe, qw, se, sw, gn, gs, hn, hs,
    load_sem, send_sem, recv_sem, ready,
):
    levels, rows, columns = t_v.shape
    own_top = PAD + HALO
    top = own_top + rows
    ext = rows + 2 * HALO
    x_v = (x_0, x_1, x_2)
    lat, lon = lax.axis_index("lat"), lax.axis_index("lon")
    last, first = lat == n_lat - 1, lat == 0
    not_last, not_first = lat < n_lat - 1, lat > 0
    east, west = lax.rem(lon + 1, n_lon), lax.rem(lon + n_lon - 1, n_lon)
    mirror = n_lon - 1 - lon
    fold_e = lax.rem(2 * n_lon - 2 - lon, n_lon)
    fold_w = lax.rem(n_lon - lon, n_lon)

    low, own, high = pl.ds(PAD, HALO), pl.ds(own_top, rows), pl.ds(top, HALO)
    own_low, own_high = pl.ds(own_top, HALO), pl.ds(top - HALO, HALO)
    part_low, part_high = pl.ds(0, HALO), pl.ds(rows - HALO, HALO)
    edge_low, middle, edge_high = pl.ds(0, HALO), pl.ds(HALO, rows), pl.ds(HALO + rows, HALO)
    halves = (pl.ds(0, 128), pl.ds(128, 128))
    inner = pl.ds(0, 2)

    loads = [
        (th, h_v), (mk, m_v), (zu, u_v), (mv, v_v), (tr, t_v),
    ]
    for f, field in enumerate((sf, zb, mb)):
        for t in range(2):
            loads.append((field.at[:, halves[t]], x_v[f].at[t, own, :]))
    loads = [pltpu.make_async_copy(s, d, load_sem.at[i]) for i, (s, d) in enumerate(loads)]

    always = lat >= 0
    partners = {
        N: (lat + 1, lon, not_last),
        S: (lat - 1, lon, not_first),
        E: (lat, east, always),
        W: (lat, west, always),
        NE: (lat + 1, east, not_last),
        NW: (lat + 1, west, not_last),
        SE: (lat - 1, east, not_first),
        SW: (lat - 1, west, not_first),
        FOLD: (lat, mirror, last),
        FOLD_E: (lat, fold_e, last & (fold_e != lon)),
        FOLD_W: (lat, fold_w, last & (fold_w != lon)),
    }

    def order(some_lat, some_lon):
        ring = lax.rem(some_lat, RING)
        ring = jnp.where(ring < RING // 2, ring, RING + RING // 2 - 1 - ring)
        turn = lax.div(some_lat, RING)
        place = 4 * ring + 5 * turn + 13 * lax.div(some_lon, 2)
        near = 4 * (RING // 2) + 5 * ((n_lat - 1) // RING) + 13 * (n_lon // 4 - 1)
        far = (some_lat == n_lat - 1) & (some_lon >= n_lon // 2)
        return jnp.where(
            far, (near + 1) * n_lon + n_lon - 1 - some_lon, place * n_lon + some_lon
        )

    mine = order(lat, lon)
    later = {p: order(*at[:2]) > mine for p, at in partners.items()}

    def is_later(p):
        return partners[p][2] & later[p]

    def is_earlier(p):
        return partners[p][2] & jnp.logical_not(later[p])

    barrier = pltpu.get_barrier_semaphore()
    for p in (W, NW, SW, FOLD, FOLD_E, FOLD_W, N, S, E, NE, SE):

        @pl.when(is_later(p))
        def _():
            pl.semaphore_signal(
                barrier, inc=1, device_id=partners[p][:2], device_id_type=MESH
            )

    for load in loads:
        load.start()

    def send(src, dst, out_slot, in_slot, to_lat, to_lon):
        return pltpu.make_async_remote_copy(
            src_ref=src, dst_ref=dst, send_sem=send_sem.at[out_slot],
            recv_sem=recv_sem.at[in_slot], device_id=(to_lat, to_lon), device_id_type=MESH,
        )

    def arrived(dst, in_slot):
        send(dst, dst, 0, in_slot, lat, east).wait_recv()

    def sent(src, out_slot):
        send(src, src, out_slot, 0, lat, east).wait_send()


    state = (sf, zb, mb)

    def start(p, src, dst, out_slot, in_slot):
        send(src, dst, out_slot, in_slot, *partners[p][:2]).start()

    def send_state(p):
        rows_out = part_low if p == S else part_high
        rows_in = low if p == N else high
        out_slot, in_slot = DN_ST if p == S else UP_ST, ST_S if p == N else ST_N
        for f in range(3):
            for t in range(2):
                slot = 2 * f + t
                start(
                    p, state[f].at[rows_out, halves[t]], x_v[f].at[t, rows_in, :],
                    out_slot + slot, in_slot + slot,
                )

    def send_column(p):
        rows_out = own_low if p == S else own_high
        rows_in = low if p == N else high
        start(
            p, f_v.at[:, inner, rows_out, :], f_v.at[:, inner, rows_in, :],
            DN_CF if p == S else UP_CF, CF_S if p == N else CF_N,
        )

    sides = {
        E: (pe, rw.at[middle], SD_E, P_W),
        W: (pw, re.at[middle], SD_W, P_E),
        NE: (pe.at[part_high], rw.at[edge_low], SD_EU, P_SW),
        NW: (pw.at[part_high], re.at[edge_low], SD_WU, P_SE),
        SE: (pe.at[part_low], rw.at[edge_high], SD_ED, P_NW),
        SW: (pw.at[part_low], re.at[edge_high], SD_WD, P_NE),
        FOLD_E: (pe.at[part_high], re.at[edge_high], SD_EU, P_NE),
        FOLD_W: (pw.at[part_high], rw.at[edge_high], SD_WU, P_NW),
    }
    tracers = {
        N: (gn, hs, SD_TU, T_S),
        S: (gs, hn, SD_TD, T_N),
        E: (qe, sw, SD_TE, T_W),
        W: (qw, se, SD_TW, T_E),
        FOLD: (gn, hn, SD_TU, T_N),
    }

    def send_flat(p):
        if p in sides:
            start(p, *sides[p])
        else:
            send_column(p)

    def send_to_later(group):
        for p in group:

            @pl.when(is_later(p))
            def _():
                pl.semaphore_wait(ready.at[p], 1)
                if p not in sides:
                    send_state(p)
                send_flat(p)
                if p in tracers:
                    start(p, *tracers[p])

    count = sum(jnp.where(is_earlier(p), 1, 0) for p in partners)

    def greeted():
        @pl.when(count > 0)
        def _():
            pl.semaphore_wait(barrier, count)

        for p in (E, NE, SE, FOLD, FOLD_E, FOLD_W, W, NW, SW, S, N):

            @pl.when(is_earlier(p))
            def _():
                pl.semaphore_signal(
                    ready.at[OPPOSITE[p]], inc=1, device_id=partners[p][:2],
                    device_id_type=MESH,
                )

    @pl.when(last)
    def _():
        greeted()

        @pl.when(is_earlier(FOLD))
        def _():
            send_state(FOLD)

    for load in loads[:4]:
        load.wait()

    @pl.when(not_last)
    def _():
        greeted()

    for p in (N, S):

        @pl.when(is_earlier(p))
        def _():
            send_state(p)

    def add_level(k, sums):
        wet = m_v[k].astype(jnp.float32) * h_v[k]
        w_v[k] = wet
        return sums[0] + wet, sums[1] + wet * u_v[k], sums[2] + wet * v_v[k]

    zero = jnp.zeros((rows, columns), jnp.float32)
    depth, force_u, force_v = lax.fori_loop(0, levels, add_level, (zero, zero, zero))
    force_u, force_v = 0.05 * force_u, 0.05 * force_v
    for t in range(2):
        f_v[0, t, own, :] = depth[:, 128 * t : 128 * t + 128]
    for t in range(2):
        f_v[1, t, own, :] = force_u[:, 128 * t : 128 * t + 128]
    for t in range(2):
        f_v[2, t, own, :] = force_v[:, 128 * t : 128 * t + 128]

    for load in loads[4:]:
        load.wait()

    lane = lanes((rows, 128))
    firsts = [x_v[f][0, own, :] for f in range(3)]
    lasts = [x_v[f][1, own, :] for f in range(3)]
    for total in (depth, force_u, force_v):
        firsts.append(total[:, :128])
        lasts.append(total[:, columns - 128 :])
    pack_e = jnp.zeros((rows, 128), jnp.float32)
    pack_w = jnp.zeros((rows, 128), jnp.float32)
    for f in range(6):
        here = (lane >= HALO * f) & (lane < HALO * (f + 1))
        from_e = pltpu.roll(lasts[f], (HALO * f + HALO) % 128, 1)
        pack_e = jnp.where(here, from_e, pack_e)
        from_w = firsts[f]
        if f:
            from_w = pltpu.roll(from_w, HALO * f, 1)
        pack_w = jnp.where(here, from_w, pack_w)
    pe[...] = pack_e
    pw[...] = pack_w
    for p in (E, NE, SE, FOLD, S, N, FOLD_E, FOLD_W, W, NW, SW):

        @pl.when(is_earlier(p))
        def _():
            send_flat(p)

    @pl.when(last & (fold_e == lon))
    def _():
        pltpu.make_async_copy(pe.at[part_high], re.at[edge_high], recv_sem.at[P_NE]).start()

    @pl.when(last & (fold_w == lon))
    def _():
        pltpu.make_async_copy(pw.at[part_high], rw.at[edge_high], recv_sem.at[P_NW]).start()


    pack_e = jnp.zeros((rows, 128), jnp.float32)
    pack_w = jnp.zeros((rows, 128), jnp.float32)
    for i, source in enumerate((t_v, w_v, u_v)):
        for k in range(levels):
            slot = i * levels + k
            pack_e = jnp.where(
                lane == slot, pltpu.roll(source[k, :, columns - 128 :], slot + 1, 1), pack_e
            )
            from_w = source[k, :, :128]
            if slot:
                from_w = pltpu.roll(from_w, slot, 1)
            pack_w = jnp.where(lane == slot, from_w, pack_w)
    qe[...] = pack_e
    qw[...] = pack_w
    for i, source in enumerate((t_v, w_v, v_v)):
        gn[i] = source[:, rows - 1, :]
        gs[i] = source[:, 0, :]
    for p in (E, FOLD, S, N, W):

        @pl.when(is_earlier(p))
        def _():
            start(p, *tracers[p])

    send_to_later((N, S, E, NE, SE))

    col = lanes((rows, columns))
    row = lax.broadcasted_iota(jnp.int32, (rows, columns), 0)

    def tracer_level(k, lower):
        t, w, u, v = t_v[k], w_v[k], u_v[k], v_v[k]
        t_e, w_e, u_e = (pltpu.roll(z, columns - 1, 1) for z in (t, w, u))
        flux = jnp.minimum(w, w_e) * (0.25 * (u + u_e) * (t + t_e) - 0.1 * (t_e - t))
        flux = jnp.where(col == columns - 1, 0.0, flux)
        flow = flux - pltpu.roll(flux, 1, 1)
        t_n, w_n, v_n = (pltpu.roll(z, rows - 1, 0) for z in (t, w, v))
        flux = jnp.minimum(w, w_n) * (0.25 * (v + v_n) * (t + t_n) - 0.1 * (t_n - t))
        flux = jnp.where(row == rows - 1, 0.0, flux)
        flow = flow + (flux - pltpu.roll(flux, 1, 0))
        above = jnp.minimum(k + 1, levels - 1)
        upper = 0.2 * jnp.minimum(w, w_v[above]) * (t_v[above] - t)
        scale = 0.2 * m_v[k].astype(jnp.float32) / h_v[k]
        c_v[k] = scale
        out_v[k] = t + scale * ((upper - lower) - flow)
        return upper

    lax.fori_loop(0, levels, tracer_level, zero)
    send_to_later((W, NW, SW, FOLD, FOLD_E, FOLD_W))

    def face(t_a, t_b, w_a, w_b, u_a, u_b):
        return jnp.minimum(w_a, w_b) * (0.25 * (u_a + u_b) * (t_a + t_b) - 0.1 * (t_b - t_a))

    def packed_face(a, b):
        a_1, b_1 = pltpu.roll(a, 128 - levels, 1), pltpu.roll(b, 128 - levels, 1)
        a_2, b_2 = pltpu.roll(a, 128 - 2 * levels, 1), pltpu.roll(b, 128 - 2 * levels, 1)
        return face(a, b, a_1, b_1, a_2, b_2)

    lane = lanes((rows, 128))
    arrived(se, T_E)

    @pl.when(not_first)
    def _():
        arrived(hs, T_S)

    @pl.when(first)
    def _():
        hs[...] = jnp.zeros(hs.shape, jnp.float32)

    flux_e = packed_face(qe[...], se[...])
    for k in range(levels):
        edge = halves[1]
        moved = pltpu.roll(flux_e, 127 - k, 1)
        out_v[k, :, edge] = out_v[k, :, edge] - jnp.where(
            lane == 127, c_v[k, :, edge] * moved, 0.0
        )
    flux_s = face(hs[0], gs[0], hs[1], gs[1], hs[2], gs[2])
    out_v[:, 0, :] = out_v[:, 0, :] + c_v[:, 0, :] * flux_s

    for f in range(3):
        for t in range(2):
            arrived(x_v[f].at[t, high, :], ST_N + 2 * f + t)
    arrived(f_v.at[:, inner, high, :], CF_N)
    arrived(re.at[middle], P_E)
    arrived(rw.at[middle], P_W)
    arrived(re.at[edge_high], P_NE)
    arrived(rw.at[edge_high], P_NW)

    @pl.when(not_first)
    def _():
        for f in range(3):
            for t in range(2):
                arrived(x_v[f].at[t, low, :], ST_S + 2 * f + t)
        arrived(f_v.at[:, inner, low, :], CF_S)
        arrived(re.at[edge_low], P_SE)
        arrived(rw.at[edge_low], P_SW)

    @pl.when(first)
    def _():
        f_v[:, inner, low, :] = jnp.zeros((3, 2, HALO, 128), jnp.float32)
        for f in range(3):
            x_v[f][inner, low, :] = jnp.zeros((2, HALO, 128), jnp.float32)
        re[edge_low] = jnp.zeros((HALO, 128), jnp.float32)
        rw[edge_low] = jnp.zeros((HALO, 128), jnp.float32)

    @pl.when(last)
    def _():
        for f in range(6):
            ref = x_v[f] if f < 3 else f_v.at[f - 3]
            old = [ref[t, high, :] for t in range(2)]
            for t in range(2):
                new = flip_lanes(flip_rows(old[1 - t]), 127)
                ref[t, high, :] = new if f % 3 == 0 else -new
        field = lanes((HALO, 128)) // HALO
        even = (field == 0) | (field == 3)
        for ref in (re, rw):
            new = flip_lanes(flip_rows(ref[edge_high]), HALO - 1)
            ref[edge_high] = jnp.where(even, new, -new)

    span = pl.ds(PAD, ext)
    lane = lanes((ext, 128))
    from_e, from_w = re[...], rw[...]
    for f in range(6):
        shift = (128 - HALO * f) % 128
        tile_e = pltpu.roll(from_e, shift, 1) if shift else from_e
        shift = 128 - HALO - HALO * f
        tile_w = pltpu.roll(from_w, shift, 1) if shift else from_w
        ref = x_v[f] if f < 3 else f_v.at[f - 3]
        ref[2, span, :] = jnp.where(lane < 64, tile_e, tile_w)

    def to_east_of(tiles):
        turned = [pltpu.roll(x, 127, 1) for x in tiles]
        edge = lanes(tiles[0].shape) == 127
        return [jnp.where(edge, turned[(t + 1) % 3], turned[t]) for t in range(3)]

    def to_west_of(tiles):
        turned = [pltpu.roll(x, 1, 1) for x in tiles]
        edge = lanes(tiles[0].shape) == 0
        return [jnp.where(edge, turned[(t + 2) % 3], turned[t]) for t in range(3)]

    for r in range(PAD, PAD + ext, HALO):
        here, north = pl.ds(r, HALO), pl.ds(r + 1, HALO)
        d = [f_v[0, t, here, :] for t in range(3)]
        d_e, d_w = to_east_of(d), to_west_of(d)
        for t in range(3):
            wet = jnp.minimum(2.0 * d[t], 1.0)
            a_v[0, t, here, :] = wet
            a_v[1, t, here, :] = 0.01 * wet
            a_v[2, t, here, :] = 0.5 * jnp.minimum(d[t], d_e[t])
            a_v[6, t, here, :] = 0.5 * jnp.minimum(d[t], d_w[t])
            a_v[3, t, here, :] = 0.5 * jnp.minimum(d[t], f_v[0, t, north, :])
            a_v[4, t, here, :] = 0.2 * f_v[1, t, here, :]
            a_v[5, t, here, :] = 0.2 * f_v[2, t, here, :]
            x_v[0][t, here, :] = 0.05 * x_v[0][t, here, :]

    def heights(r):
        here, north, south = pl.ds(r, CHUNK), pl.ds(r + 1, CHUNK), pl.ds(r - 1, CHUNK)
        ub = [x_1[t, here, :] for t in range(3)]
        ub_e, ub_w = to_east_of(ub), to_west_of(ub)
        for t in range(3):
            vb = x_2[t, here, :]
            out_n = a_v[3, t, here, :] * (vb + x_2[t, north, :])
            in_s = a_v[3, t, south, :] * (vb + x_2[t, south, :])
            out_e = a_v[2, t, here, :] * (ub[t] + ub_e[t])
            in_w = a_v[6, t, here, :] * (ub[t] + ub_w[t])
            div = (out_e - in_w) + (out_n - in_s)
            x_0[t, here, :] = x_0[t, here, :] - a_v[1, t, here, :] * div

    def speeds(r):
        here, north, south = pl.ds(r, CHUNK), pl.ds(r + 1, CHUNK), pl.ds(r - 1, CHUNK)
        eta = [x_0[t, here, :] for t in range(3)]
        eta_e, eta_w = to_east_of(eta), to_west_of(eta)
        for t in range(3):
            wet = a_v[0, t, here, :]
            drive = a_v[4, t, here, :] - (eta_e[t] - eta_w[t])
            x_1[t, here, :] = wet * (x_1[t, here, :] + drive)
            slope = x_0[t, north, :] - x_0[t, south, :]
            drive = a_v[5, t, here, :] - slope
            x_2[t, here, :] = wet * (x_2[t, here, :] + drive)

    def cycles(start_row, count):
        def step(_, carry):
            for r in range(start_row, start_row + count, CHUNK):
                heights(r)
                if r > start_row:
                    speeds(r - CHUNK)
            speeds(start_row + count - CHUNK)
            return carry

        lax.fori_loop(0, SUB // 2, step, 0, unroll=True)

    cycles(PAD, ext)
    cycles(PAD + SUB, ext - HALO)
    for t in range(2):
        o_st[0, :, halves[t]] = 20.0 * x_v[0][t, own, :]
        for f in range(1, 3):
            o_st[f, :, halves[t]] = x_v[f][t, own, :]

    arrived(hn, T_N)
    arrived(sw, T_W)

    @pl.when(last)
    def _():
        for i in range(3):
            old = hn[i]
            tiles = [old[:, c : c + 128] for c in range(columns - 128, -128, -128)]
            new = jnp.concatenate([flip_lanes(t, 127) for t in tiles], axis=1)
            hn[i] = -new if i == 2 else new

    flux_w = packed_face(sw[...], qw[...])
    for k in range(levels):
        edge = halves[0]
        moved = pltpu.roll(flux_w, 128 - k, 1) if k else flux_w
        out_v[k, :, edge] = out_v[k, :, edge] + jnp.where(
            lanes((rows, 128)) == 0, c_v[k, :, edge] * moved, 0.0
        )
    flux_n = face(gn[0], hn[0], gn[1], hn[1], gn[2], hn[2])
    out_v[:, rows - 1, :] = out_v[:, rows - 1, :] - c_v[:, rows - 1, :] * flux_n

    for slot in range(6):
        sent(sf.at[part_low, halves[0]], UP_ST + slot)
    sent(f_v.at[:, inner, own_low, :], UP_CF)
    sent(pe, SD_E)
    sent(pw, SD_W)
    sent(gn, SD_TU)
    sent(qe, SD_TE)
    sent(qw, SD_TW)

    @pl.when(not_last | (fold_e != lon))
    def _():
        sent(pe.at[part_high], SD_EU)

    @pl.when(not_last | (fold_w != lon))
    def _():
        sent(pw.at[part_high], SD_WU)

    @pl.when(not_first)
    def _():
        for slot in range(6):
            sent(sf.at[part_low, halves[0]], DN_ST + slot)
        sent(f_v.at[:, inner, own_low, :], DN_CF)
        sent(pe.at[part_low], SD_ED)
        sent(pw.at[part_low], SD_WD)
        sent(gs, SD_TD)


def store_kernel(tr, st, o_tr, o_sf, o_zb, o_mb, sem):
    copies = [pltpu.make_async_copy(tr, o_tr, sem.at[3])]
    for f, dst in enumerate((o_sf, o_zb, o_mb)):
        copies.append(pltpu.make_async_copy(st.at[f], dst, sem.at[f]))
    for copy in copies:
        copy.start()
    for copy in copies:
        copy.wait()


def on_device(n_lat, n_lon, *args):
    levels, rows, columns = args[0].shape
    block = pltpu.VMEM((levels, rows, columns), jnp.float32)
    ext, wide = rows + 2 * HALO, columns // 128 + 1
    strip, long_strip = pltpu.VMEM((rows, 128), jnp.float32), pltpu.VMEM((ext, 128), jnp.float32)
    line = pltpu.VMEM((3, levels, columns), jnp.float32)
    tiles = (wide, ext + 2 * PAD, 128)
    scratch = [block, block, pltpu.VMEM((levels, rows, columns), jnp.int32)] + [block] * 4
    scratch += [pltpu.VMEM(tiles, jnp.float32)] * 3
    scratch += [pltpu.VMEM((n, *tiles), jnp.float32) for n in (3, 7)]
    scratch += [strip] * 2 + [long_strip] * 2 + [strip] * 4 + [line] * 4
    scratch += [
        pltpu.SemaphoreType.DMA((11,)),
        pltpu.SemaphoreType.DMA((SLOTS,)), pltpu.SemaphoreType.DMA((SLOTS,)),
        pltpu.SemaphoreType.REGULAR((11,)),
    ]
    whole = jax.ShapeDtypeStruct((levels, rows, columns), jnp.float32)
    surface = jax.ShapeDtypeStruct((rows, columns), jnp.float32)
    in_vmem = pl.BlockSpec(memory_space=pltpu.VMEM)
    anywhere = pl.BlockSpec(memory_space=pl.ANY)
    args = [pltpu.with_memory_space_constraint(a, pltpu.HBM) for a in args]
    tracer, state = pl.pallas_call(
        functools.partial(kernel, n_lat, n_lon),
        out_shape=(whole, jax.ShapeDtypeStruct((3, rows, columns), jnp.float32)),
        in_specs=[anywhere] * 8,
        out_specs=(in_vmem,) * 2,
        scratch_shapes=scratch,
        compiler_params=pltpu.CompilerParams(
            collective_id=0, has_side_effects=True, vmem_limit_bytes=32 << 20
        ),
        name="ocean",
    )(*args)
    return pl.pallas_call(
        store_kernel,
        out_shape=(whole, surface, surface, surface),
        in_specs=[in_vmem] * 2,
        out_specs=(anywhere,) * 4,
        scratch_shapes=[pltpu.SemaphoreType.DMA((4,))],
        compiler_params=pltpu.CompilerParams(vmem_limit_bytes=32 << 20),

        name="store",
    )(tracer, state)


def solution(mesh):
    whole, surface = P(None, "lat", "lon"), P("lat", "lon")
    return jax.shard_map(
        functools.partial(on_device, mesh.shape["lat"], mesh.shape["lon"]),
        mesh=mesh,
        in_specs=(whole,) * 5 + (surface,) * 3,
        out_specs=(whole, surface, surface, surface),
        check_vma=False,
    )
```

time: 23.4 us -> 21.4 us (0.915)
  Pallas kernels: 22.6 us -> 20.6 us
    pallas_call x1, Pallas kernels: 21.9 us -> 19.8 us  [on_device(): pl.pallas_call(functools.partial(kernel, n_lat, n_lon), out_shape=(whole,...]
where the time goes in v3:
time: 21.4 us; the launch traced here: 21.2 us
  Pallas kernels  20.6 us (96%)
  between operations  0.64 us (3%)
    pallas_call x1, Pallas kernels, on_device(): pl.pallas_call(functools.partial(kernel, n_lat, n_lon), out_shape=(whole,...  19.8 us
    pallas_call x1, Pallas kernels, on_device(): pl.pallas_call(store_kernel, out_shape=(whole, surface, surface, surface)...  0.76 us

profile of v3, /device:TPU:63, one launch (start us, length us, event | category | flops | bytes accessed | tf_op | source)
XLA Modules:
  0.0 21.2 jit_solution(14454542169080936066)
XLA Ops:
  0.6 19.8 %ocean.1 = (f32[8,32,256]{2,1,0:T(8,128)S(1)}, f32[3,32,256]{2,1,0:T(8,128)S(1)}) custom-call(f32[8,32,256]{2,1,0:T(8,128)} %tr.1, f32[8,32,256]{2,1,0:T(8,128)} %th.1, s32[8,32,256]{2,1,0:T(8,128)} %mk.1, f32[8,32,256]{2,1,0:T(8,128)} %zu.1, f32[8,32,256]{2,1,0:T(8,128)} %mv.1, f32[32,256]{1,0:T(8,128)} %sf.1, f32[32,256]{1,0:T(8,128)} %zb.1, f32[32,256]{1,0:T(8,128)} %mb.1), custom_call_target="tpu_custom_call" | custom-call | tf_op jit(solution)/shard_map/ocean/pallas_call | solution.py:569
  20.5 0.8 %store.1 = (f32[8,32,256]{2,1,0:T(8,128)}, f32[32,256]{1,0:T(8,128)}, f32[32,256]{1,0:T(8,128)}, f32[32,256]{1,0:T(8,128)}) custom-call(f32[8,32,256]{2,1,0:T(8,128)S(1)} %get-tuple-element.6.tr, f32[3,32,256]{2,1,0:T(8,128)S(1)} %get-tuple-element.7.st), custom_call_target="tpu_custom_call" | custom-call | tf_op jit(solution)/shard_map/store/pallas_call | solution.py:580

commit v4 on v3

--- a/solution.py
+++ b/solution.py
@@ -104,9 +104,8 @@
         place = 4 * ring + 5 * turn + 13 * lax.div(some_lon, 2)
         near = 4 * (RING // 2) + 5 * ((n_lat - 1) // RING) + 13 * (n_lon // 4 - 1)
         far = (some_lat == n_lat - 1) & (some_lon >= n_lon // 2)
-        return jnp.where(
-            far, (near + 1) * n_lon + n_lon - 1 - some_lon, place * n_lon + some_lon
-        )
+        swapped = some_lon + 1 - 2 * lax.rem(some_lon, 2)
+        return jnp.where(far, near + 1, place) * n_lon + swapped
 
     mine = order(lat, lon)
     later = {p: order(*at[:2]) > mine for p, at in partners.items()}
@@ -227,6 +226,8 @@
         def _():
             send_state(FOLD)
 
+    in_front = lax.div(mirror, 2) != 1
+
     for load in loads[:4]:
         load.wait()
 
@@ -257,6 +258,10 @@
 
     for load in loads[4:]:
         load.wait()
+
+    @pl.when(is_earlier(FOLD) & in_front)
+    def _():
+        send_column(FOLD)
 
     lane = lanes((rows, 128))
     firsts = [x_v[f][0, own, :] for f in range(3)]
@@ -276,11 +281,17 @@
         pack_w = jnp.where(here, from_w, pack_w)
     pe[...] = pack_e
     pw[...] = pack_w
-    for p in (E, NE, SE, FOLD, S, N, FOLD_E, FOLD_W, W, NW, SW):
+    for p in (E, NE, SE, FOLD_E, FOLD_W, W, NW, SW):
 
         @pl.when(is_earlier(p))
         def _():
-            send_flat(p)
+            start(p, *sides[p])
+
+    for p in (S, N):
+
+        @pl.when(is_earlier(p))
+        def _():
+            send_column(p)
 
     @pl.when(last & (fold_e == lon))
     def _():
@@ -309,8 +320,9 @@
         gn[i] = source[:, rows - 1, :]
         gs[i] = source[:, 0, :]
     for p in (E, FOLD, S, N, W):
-
-        @pl.when(is_earlier(p))
+        now = is_earlier(p) & in_front if p == FOLD else is_earlier(p)
+
+        @pl.when(now)
         def _():
             start(p, *tracers[p])
 
@@ -337,7 +349,13 @@
         return upper
 
     lax.fori_loop(0, levels, tracer_level, zero)
-    send_to_later((W, NW, SW, FOLD, FOLD_E, FOLD_W))
+
+    @pl.when(is_earlier(FOLD) & jnp.logical_not(in_front))
+    def _():
+        send_column(FOLD)
+        start(FOLD, *tracers[FOLD])
+
+    send_to_later((FOLD, FOLD_E, FOLD_W, W, NW, SW))
 
     def face(t_a, t_b, w_a, w_b, u_a, u_b):
         return jnp.minimum(w_a, w_b) * (0.25 * (u_a + u_b) * (t_a + t_b) - 0.1 * (t_b - t_a))
@@ -371,6 +389,18 @@
     for f in range(3):
         for t in range(2):
             arrived(x_v[f].at[t, high, :], ST_N + 2 * f + t)
+
+    def flip_north(refs):
+        for f, ref in enumerate(refs):
+            old = [ref[t, high, :] for t in range(2)]
+            for t in range(2):
+                new = flip_lanes(flip_rows(old[1 - t]), 127)
+                ref[t, high, :] = new if f == 0 else -new
+
+    @pl.when(last)
+    def _():
+        flip_north(x_v)
+
     arrived(f_v.at[:, inner, high, :], CF_N)
     arrived(re.at[middle], P_E)
     arrived(rw.at[middle], P_W)
@@ -396,12 +426,7 @@
 
     @pl.when(last)
     def _():
-        for f in range(6):
-            ref = x_v[f] if f < 3 else f_v.at[f - 3]
-            old = [ref[t, high, :] for t in range(2)]
-            for t in range(2):
-                new = flip_lanes(flip_rows(old[1 - t]), 127)
-                ref[t, high, :] = new if f % 3 == 0 else -new
+        flip_north([f_v.at[f] for f in range(3)])
         field = lanes((HALO, 128)) // HALO
         even = (field == 0) | (field == 3)
         for ref in (re, rw):

time: 21.4 us -> 20.1 us (0.939)
  Pallas kernels: 20.6 us -> 19.3 us
    pallas_call x1, Pallas kernels: 19.8 us -> 18.5 us  [on_device(): pl.pallas_call(functools.partial(kernel, n_lat, n_lon), out_shape=(whole,...]
where the time goes in v4:
time: 20.1 us; the launch traced here: 19.9 us
  Pallas kernels  19.3 us (96%)
  between operations  0.64 us (3%)
    pallas_call x1, Pallas kernels, on_device(): pl.pallas_call(functools.partial(kernel, n_lat, n_lon), out_shape=(whole,...  18.5 us
    pallas_call x1, Pallas kernels, on_device(): pl.pallas_call(store_kernel, out_shape=(whole, surface, surface, surface)...  0.76 us

profile of v4, /device:TPU:63, one launch (start us, length us, event | category | flops | bytes accessed | tf_op | source)
XLA Modules:
  0.0 19.9 jit_solution(10349853279140468892)
XLA Ops:
  0.6 18.5 %ocean.1 = (f32[8,32,256]{2,1,0:T(8,128)S(1)}, f32[3,32,256]{2,1,0:T(8,128)S(1)}) custom-call(f32[8,32,256]{2,1,0:T(8,128)} %tr.1, f32[8,32,256]{2,1,0:T(8,128)} %th.1, s32[8,32,256]{2,1,0:T(8,128)} %mk.1, f32[8,32,256]{2,1,0:T(8,128)} %zu.1, f32[8,32,256]{2,1,0:T(8,128)} %mv.1, f32[32,256]{1,0:T(8,128)} %sf.1, f32[32,256]{1,0:T(8,128)} %zb.1, f32[32,256]{1,0:T(8,128)} %mb.1), custom_call_target="tpu_custom_call" | custom-call | tf_op jit(solution)/shard_map/ocean/pallas_call | solution.py:594
  19.1 0.8 %store.1 = (f32[8,32,256]{2,1,0:T(8,128)}, f32[32,256]{1,0:T(8,128)}, f32[32,256]{1,0:T(8,128)}, f32[32,256]{1,0:T(8,128)}) custom-call(f32[8,32,256]{2,1,0:T(8,128)S(1)} %get-tuple-element.6.tr, f32[3,32,256]{2,1,0:T(8,128)S(1)} %get-tuple-element.7.st), custom_call_target="tpu_custom_call" | custom-call | tf_op jit(solution)/shard_map/store/pallas_call | solution.py:605

commit v5 on v4

--- a/solution.py
+++ b/solution.py
@@ -81,6 +81,8 @@
         for t in range(2):
             loads.append((field.at[:, halves[t]], x_v[f].at[t, own, :]))
     loads = [pltpu.make_async_copy(s, d, load_sem.at[i]) for i, (s, d) in enumerate(loads)]
+    for load in loads:
+        load.start()
 
     always = lat >= 0
     partners = {
@@ -124,9 +126,6 @@
             pl.semaphore_signal(
                 barrier, inc=1, device_id=partners[p][:2], device_id_type=MESH
             )
-
-    for load in loads:
-        load.start()
 
     def send(src, dst, out_slot, in_slot, to_lat, to_lon):
         return pltpu.make_async_remote_copy(
@@ -256,12 +255,12 @@
     for t in range(2):
         f_v[2, t, own, :] = force_v[:, 128 * t : 128 * t + 128]
 
+    @pl.when(is_earlier(FOLD) & in_front)
+    def _():
+        send_column(FOLD)
+
     for load in loads[4:]:
         load.wait()
-
-    @pl.when(is_earlier(FOLD) & in_front)
-    def _():
-        send_column(FOLD)
 
     lane = lanes((rows, 128))
     firsts = [x_v[f][0, own, :] for f in range(3)]
@@ -281,7 +280,7 @@
         pack_w = jnp.where(here, from_w, pack_w)
     pe[...] = pack_e
     pw[...] = pack_w
-    for p in (E, NE, SE, FOLD_E, FOLD_W, W, NW, SW):
+    for p in (FOLD_E, FOLD_W, E, NE, SE, W, NW, SW):
 
         @pl.when(is_earlier(p))
         def _():
@@ -386,26 +385,17 @@
     flux_s = face(hs[0], gs[0], hs[1], gs[1], hs[2], gs[2])
     out_v[:, 0, :] = out_v[:, 0, :] + c_v[:, 0, :] * flux_s
 
-    for f in range(3):
-        for t in range(2):
-            arrived(x_v[f].at[t, high, :], ST_N + 2 * f + t)
-
-    def flip_north(refs):
-        for f, ref in enumerate(refs):
-            old = [ref[t, high, :] for t in range(2)]
-            for t in range(2):
-                new = flip_lanes(flip_rows(old[1 - t]), 127)
-                ref[t, high, :] = new if f == 0 else -new
-
-    @pl.when(last)
-    def _():
-        flip_north(x_v)
-
-    arrived(f_v.at[:, inner, high, :], CF_N)
+    arrived(sw, T_W)
+    flux_w = packed_face(sw[...], qw[...])
+    for k in range(levels):
+        edge = halves[0]
+        moved = pltpu.roll(flux_w, 128 - k, 1) if k else flux_w
+        out_v[k, :, edge] = out_v[k, :, edge] + jnp.where(
+            lanes((rows, 128)) == 0, c_v[k, :, edge] * moved, 0.0
+        )
+
     arrived(re.at[middle], P_E)
     arrived(rw.at[middle], P_W)
-    arrived(re.at[edge_high], P_NE)
-    arrived(rw.at[edge_high], P_NW)
 
     @pl.when(not_first)
     def _():
@@ -424,25 +414,16 @@
         re[edge_low] = jnp.zeros((HALO, 128), jnp.float32)
         rw[edge_low] = jnp.zeros((HALO, 128), jnp.float32)
 
-    @pl.when(last)
-    def _():
-        flip_north([f_v.at[f] for f in range(3)])
-        field = lanes((HALO, 128)) // HALO
-        even = (field == 0) | (field == 3)
-        for ref in (re, rw):
-            new = flip_lanes(flip_rows(ref[edge_high]), HALO - 1)
-            ref[edge_high] = jnp.where(even, new, -new)
-
-    span = pl.ds(PAD, ext)
-    lane = lanes((ext, 128))
-    from_e, from_w = re[...], rw[...]
-    for f in range(6):
-        shift = (128 - HALO * f) % 128
-        tile_e = pltpu.roll(from_e, shift, 1) if shift else from_e
-        shift = 128 - HALO - HALO * f
-        tile_w = pltpu.roll(from_w, shift, 1) if shift else from_w
-        ref = x_v[f] if f < 3 else f_v.at[f - 3]
-        ref[2, span, :] = jnp.where(lane < 64, tile_e, tile_w)
+    def join_sides(first_row, count):
+        lane = lanes((count, 128))
+        from_e, from_w = re[pl.ds(first_row, count)], rw[pl.ds(first_row, count)]
+        for f in range(6):
+            shift = (128 - HALO * f) % 128
+            tile_e = pltpu.roll(from_e, shift, 1) if shift else from_e
+            shift = 128 - HALO - HALO * f
+            tile_w = pltpu.roll(from_w, shift, 1) if shift else from_w
+            ref = x_v[f] if f < 3 else f_v.at[f - 3]
+            ref[2, pl.ds(PAD + first_row, count), :] = jnp.where(lane < 64, tile_e, tile_w)
 
     def to_east_of(tiles):
         turned = [pltpu.roll(x, 127, 1) for x in tiles]
@@ -454,8 +435,13 @@
         edge = lanes(tiles[0].shape) == 0
         return [jnp.where(edge, turned[(t + 2) % 3], turned[t]) for t in range(3)]
 
-    for r in range(PAD, PAD + ext, HALO):
+    def north_faces(r):
         here, north = pl.ds(r, HALO), pl.ds(r + 1, HALO)
+        for t in range(3):
+            a_v[3, t, here, :] = 0.5 * jnp.minimum(f_v[0, t, here, :], f_v[0, t, north, :])
+
+    def constants(r):
+        here = pl.ds(r, HALO)
         d = [f_v[0, t, here, :] for t in range(3)]
         d_e, d_w = to_east_of(d), to_west_of(d)
         for t in range(3):
@@ -464,10 +450,49 @@
             a_v[1, t, here, :] = 0.01 * wet
             a_v[2, t, here, :] = 0.5 * jnp.minimum(d[t], d_e[t])
             a_v[6, t, here, :] = 0.5 * jnp.minimum(d[t], d_w[t])
-            a_v[3, t, here, :] = 0.5 * jnp.minimum(d[t], f_v[0, t, north, :])
             a_v[4, t, here, :] = 0.2 * f_v[1, t, here, :]
             a_v[5, t, here, :] = 0.2 * f_v[2, t, here, :]
             x_v[0][t, here, :] = 0.05 * x_v[0][t, here, :]
+
+    join_sides(0, HALO + rows)
+    chunks = range(PAD, PAD + ext, HALO)
+    for r in chunks[:-1]:
+        constants(r)
+    for r in chunks[:-2]:
+        north_faces(r)
+
+    for f in range(3):
+        for t in range(2):
+            arrived(x_v[f].at[t, high, :], ST_N + 2 * f + t)
+
+    def flip_north(refs):
+        for f, ref in enumerate(refs):
+            old = [ref[t, high, :] for t in range(2)]
+            for t in range(2):
+                new = flip_lanes(flip_rows(old[1 - t]), 127)
+                ref[t, high, :] = new if f == 0 else -new
+
+    @pl.when(last)
+    def _():
+        flip_north(x_v)
+
+    arrived(re.at[edge_high], P_NE)
+    arrived(rw.at[edge_high], P_NW)
+    arrived(f_v.at[:, inner, high, :], CF_N)
+
+    @pl.when(last)
+    def _():
+        flip_north([f_v.at[f] for f in range(3)])
+        field = lanes((HALO, 128)) // HALO
+        even = (field == 0) | (field == 3)
+        for ref in (re, rw):
+            new = flip_lanes(flip_rows(ref[edge_high]), HALO - 1)
+            ref[edge_high] = jnp.where(even, new, -new)
+
+    join_sides(HALO + rows, HALO)
+    constants(chunks[-1])
+    north_faces(chunks[-2])
+    north_faces(chunks[-1])
 
     def heights(r):
         here, north, south = pl.ds(r, CHUNK), pl.ds(r + 1, CHUNK), pl.ds(r - 1, CHUNK)
@@ -513,7 +538,6 @@
             o_st[f, :, halves[t]] = x_v[f][t, own, :]
 
     arrived(hn, T_N)
-    arrived(sw, T_W)
 
     @pl.when(last)
     def _():
@@ -523,13 +547,6 @@
             new = jnp.concatenate([flip_lanes(t, 127) for t in tiles], axis=1)
             hn[i] = -new if i == 2 else new
 
-    flux_w = packed_face(sw[...], qw[...])
-    for k in range(levels):
-        edge = halves[0]
-        moved = pltpu.roll(flux_w, 128 - k, 1) if k else flux_w
-        out_v[k, :, edge] = out_v[k, :, edge] + jnp.where(
-            lanes((rows, 128)) == 0, c_v[k, :, edge] * moved, 0.0
-        )
     flux_n = face(gn[0], hn[0], gn[1], hn[1], gn[2], hn[2])
     out_v[:, rows - 1, :] = out_v[:, rows - 1, :] - c_v[:, rows - 1, :] * flux_n
 

time: 20.1 us -> 19.9 us (0.990)
  no operation moved by 1% of the time
where the time goes in v5:
time: 19.9 us; the launch traced here: 19.7 us
  Pallas kernels  19.1 us (96%)
  between operations  0.64 us (3%)
    pallas_call x1, Pallas kernels, on_device(): pl.pallas_call(functools.partial(kernel, n_lat, n_lon), out_shape=(whole,...  18.3 us
    pallas_call x1, Pallas kernels, on_device(): pl.pallas_call(store_kernel, out_shape=(whole, surface, surface, surface)...  0.76 us

profile of v5, /device:TPU:63, one launch (start us, length us, event | category | flops | bytes accessed | tf_op | source)
XLA Modules:
  0.0 19.7 jit_solution(13395866554432268575)
XLA Ops:
  0.6 18.3 %ocean.1 = (f32[8,32,256]{2,1,0:T(8,128)S(1)}, f32[3,32,256]{2,1,0:T(8,128)S(1)}) custom-call(f32[8,32,256]{2,1,0:T(8,128)} %tr.1, f32[8,32,256]{2,1,0:T(8,128)} %th.1, s32[8,32,256]{2,1,0:T(8,128)} %mk.1, f32[8,32,256]{2,1,0:T(8,128)} %zu.1, f32[8,32,256]{2,1,0:T(8,128)} %mv.1, f32[32,256]{1,0:T(8,128)} %sf.1, f32[32,256]{1,0:T(8,128)} %zb.1, f32[32,256]{1,0:T(8,128)} %mb.1), custom_call_target="tpu_custom_call" | custom-call | tf_op jit(solution)/shard_map/ocean/pallas_call | solution.py:611
  19.0 0.8 %store.1 = (f32[8,32,256]{2,1,0:T(8,128)}, f32[32,256]{1,0:T(8,128)}, f32[32,256]{1,0:T(8,128)}, f32[32,256]{1,0:T(8,128)}) custom-call(f32[8,32,256]{2,1,0:T(8,128)S(1)} %get-tuple-element.6.tr, f32[3,32,256]{2,1,0:T(8,128)S(1)} %get-tuple-element.7.st), custom_call_target="tpu_custom_call" | custom-call | tf_op jit(solution)/shard_map/store/pallas_call | solution.py:622

commit v6 on v5

--- a/solution.py
+++ b/solution.py
@@ -208,6 +208,7 @@
         def _():
             pl.semaphore_wait(barrier, count)
 
+    def answer():
         for p in (E, NE, SE, FOLD, FOLD_E, FOLD_W, W, NW, SW, S, N):
 
             @pl.when(is_earlier(p))
@@ -225,6 +226,8 @@
         def _():
             send_state(FOLD)
 
+        answer()
+
     in_front = lax.div(mirror, 2) != 1
 
     for load in loads[:4]:
@@ -233,6 +236,7 @@
     @pl.when(not_last)
     def _():
         greeted()
+        answer()
 
     for p in (N, S):
 

time: 19.9 us -> 19.9 us (level)
  the two profiles are of different devices: /device:TPU:63 before, /device:TPU:126 now
where the time goes in v6:
time: 19.9 us; the launch traced here: 19.7 us
  Pallas kernels  19.1 us (96%)
  between operations  0.64 us (3%)
    pallas_call x1, Pallas kernels, on_device(): pl.pallas_call(functools.partial(kernel, n_lat, n_lon), out_shape=(whole,...  18.3 us
    pallas_call x1, Pallas kernels, on_device(): pl.pallas_call(store_kernel, out_shape=(whole, surface, surface, surface)...  0.76 us

profile of v6, /device:TPU:126, one launch (start us, length us, event | category | flops | bytes accessed | tf_op | source)
XLA Modules:
  0.0 19.7 jit_solution(13597291401312420566)
XLA Ops:
  0.6 18.3 %ocean.1 = (f32[8,32,256]{2,1,0:T(8,128)S(1)}, f32[3,32,256]{2,1,0:T(8,128)S(1)}) custom-call(f32[8,32,256]{2,1,0:T(8,128)} %tr.1, f32[8,32,256]{2,1,0:T(8,128)} %th.1, s32[8,32,256]{2,1,0:T(8,128)} %mk.1, f32[8,32,256]{2,1,0:T(8,128)} %zu.1, f32[8,32,256]{2,1,0:T(8,128)} %mv.1, f32[32,256]{1,0:T(8,128)} %sf.1, f32[32,256]{1,0:T(8,128)} %zb.1, f32[32,256]{1,0:T(8,128)} %mb.1), custom_call_target="tpu_custom_call" | custom-call | tf_op jit(solution)/shard_map/ocean/pallas_call | solution.py:615
  19.0 0.8 %store.1 = (f32[8,32,256]{2,1,0:T(8,128)}, f32[32,256]{1,0:T(8,128)}, f32[32,256]{1,0:T(8,128)}, f32[32,256]{1,0:T(8,128)}) custom-call(f32[8,32,256]{2,1,0:T(8,128)S(1)} %get-tuple-element.6.tr, f32[3,32,256]{2,1,0:T(8,128)S(1)} %get-tuple-element.7.st), custom_call_target="tpu_custom_call" | custom-call | tf_op jit(solution)/shard_map/store/pallas_call | solution.py:626

commit v7 on v6

--- a/solution.py
+++ b/solution.py
@@ -358,7 +358,7 @@
         send_column(FOLD)
         start(FOLD, *tracers[FOLD])
 
-    send_to_later((FOLD, FOLD_E, FOLD_W, W, NW, SW))
+    send_to_later((W, FOLD, FOLD_E, FOLD_W, NW, SW))
 
     def face(t_a, t_b, w_a, w_b, u_a, u_b):
         return jnp.minimum(w_a, w_b) * (0.25 * (u_a + u_b) * (t_a + t_b) - 0.1 * (t_b - t_a))

time: 19.9 us -> 19.9 us (level)
  the two profiles are of different devices: /device:TPU:126 before, /device:TPU:63 now
where the time goes in v7:
time: 19.9 us; the launch traced here: 19.7 us
  Pallas kernels  19 us (95%)
  between operations  0.64 us (3%)
    pallas_call x1, Pallas kernels, on_device(): pl.pallas_call(functools.partial(kernel, n_lat, n_lon), out_shape=(whole,...  18.3 us
    pallas_call x1, Pallas kernels, on_device(): pl.pallas_call(store_kernel, out_shape=(whole, surface, surface, surface)...  0.76 us

profile of v7, /device:TPU:63, one launch (start us, length us, event | category | flops | bytes accessed | tf_op | source)
XLA Modules:
  0.0 19.7 jit_solution(3953366270289470985)
XLA Ops:
  0.6 18.3 %ocean.1 = (f32[8,32,256]{2,1,0:T(8,128)S(1)}, f32[3,32,256]{2,1,0:T(8,128)S(1)}) custom-call(f32[8,32,256]{2,1,0:T(8,128)} %tr.1, f32[8,32,256]{2,1,0:T(8,128)} %th.1, s32[8,32,256]{2,1,0:T(8,128)} %mk.1, f32[8,32,256]{2,1,0:T(8,128)} %zu.1, f32[8,32,256]{2,1,0:T(8,128)} %mv.1, f32[32,256]{1,0:T(8,128)} %sf.1, f32[32,256]{1,0:T(8,128)} %zb.1, f32[32,256]{1,0:T(8,128)} %mb.1), custom_call_target="tpu_custom_call" | custom-call | tf_op jit(solution)/shard_map/ocean/pallas_call | solution.py:615
  18.9 0.8 %store.1 = (f32[8,32,256]{2,1,0:T(8,128)}, f32[32,256]{1,0:T(8,128)}, f32[32,256]{1,0:T(8,128)}, f32[32,256]{1,0:T(8,128)}) custom-call(f32[8,32,256]{2,1,0:T(8,128)S(1)} %get-tuple-element.6.tr, f32[3,32,256]{2,1,0:T(8,128)S(1)} %get-tuple-element.7.st), custom_call_target="tpu_custom_call" | custom-call | tf_op jit(solution)/shard_map/store/pallas_call | solution.py:626
